TPU v7x, 256 devices: a whole 4x4x8 slice. The times are simulated.
256 devices in a mesh: prow: 16 (over z, core), pcol: 16 (over x, y).
Axes of the slice: x: 4, y: 4, z: 8, core: 2. Of those that a mesh axis runs over, the one named last changes fastest.
Arguments:
- tiles: bfloat16 [32768, 128, 128], P(('prow', 'pcol')), may hold values from -6 to 6
- tile_pos: int32 [32768, 2], P(('prow', 'pcol')), may hold values from -1 to 511, as said below
- pivots: int32 [2, 256], replicated, may hold values from 0 to 255, each once within a row
- inverses: bfloat16 [2, 256, 256], replicated, may hold values from -0.0234375 to 0.0234375
Outputs:
- factored: bfloat16 [32768, 128, 128], P(('prow', 'pcol'))
Inputs may be any that keep to these rules, and one draw needn't show every extreme that they name: `tile_pos`: slot s of device (p, q) (device index p * 16 + q, p along prow) holds a tile (I, J) with I % 16 == p and (J // 2) % 16 == q, or is empty; no tile is listed twice; every tile with I < 4 or J < 4 is listed; listed slots come before empty ones on each device; some device has all 128 slots listed.
All inputs are finite; a program needn't handle non-finite values.
Results may differ from a plain program's by a relative error of at most 0.0067.
Values may be sent and summed in bfloat16 or wider, within the bound.
No kernel may reach another device: no remote copies, remote signals or barrier semaphores. Data moves between devices by JAX's collectives and lax.ppermute only.
A program may use at most 128 MiB of HBM per device.

v0:
```python
import jax
import jax.numpy as jnp
from jax import lax
from jax.sharding import PartitionSpec as P

ROW_TILES = 32


def broadcast(value, axis, root):
    mine = lax.axis_index(axis) == root
    return lax.psum(jnp.where(mine, value, jnp.zeros_like(value)), axis)


def slot_lookup(keys, count):
    targets = jnp.arange(count, dtype=jnp.int32)
    matches = keys[None, :] == targets[:, None]
    positions = jnp.arange(keys.shape[0], dtype=jnp.int32)
    chosen = jnp.sum(jnp.where(matches, positions[None, :], 0), axis=1)
    found = jnp.any(matches, axis=1)
    return (chosen, found)


def local(tiles, tile_pos, pivots, inverses):
    slots, edge, _ = tiles.shape
    row_procs = lax.axis_size("prow")
    col_procs = lax.axis_size("pcol")
    my_col = lax.axis_index("pcol")
    row_tiles = ROW_TILES
    col_tiles = ROW_TILES * row_procs // col_procs
    tile_row = tile_pos[:, 0]
    tile_col = tile_pos[:, 1]
    local_row = jnp.clip(tile_row // row_procs, 0, row_tiles - 1)
    local_col = jnp.clip(2 * (tile_col // 2 // col_procs) + tile_col % 2, 0, col_tiles - 1)
    nothing = jnp.zeros((), jnp.bfloat16)
    current = tiles
    for panel in range(2):
        first = 2 * panel
        in_column = (tile_col >= first) & (tile_col < first + 2)
        col_keys = jnp.where(in_column, local_row * 2 + tile_col - first, -1)
        chosen, found = slot_lookup(col_keys, 2 * row_tiles)
        column = jnp.where(found[:, None, None], current[chosen], nothing)
        column = (
            column.reshape(row_tiles, 2, edge, edge)
            .transpose(0, 2, 1, 3)
            .reshape(row_tiles * edge, 2 * edge)
        )
        inverse = inverses[panel]

        def multiply(block):
            return jnp.dot(block, inverse, preferred_element_type=jnp.float32).astype(jnp.bfloat16)

        def blank(block):
            return jnp.zeros(block.shape, jnp.bfloat16)

        lower = lax.cond(my_col == panel, multiply, blank, column)
        lower = broadcast(lower, "pcol", panel)
        in_block = (tile_row >= first) & (tile_row < first + 2)
        row_keys = jnp.where(in_block, local_col, -1)
        chosen, found = slot_lookup(row_keys, col_tiles)
        mine = jnp.where(found[:, None, None], current[chosen], nothing)
        mine = mine.transpose(1, 0, 2).reshape(edge, col_tiles * edge)
        order = pivots[panel]
        top_rows = broadcast(mine, "prow", first)
        bottom_rows = broadcast(mine, "prow", first + 1)
        upper = jnp.concatenate([top_rows, bottom_rows], axis=0)[order]
        lower_tiles = lower.reshape(row_tiles, edge, 2 * edge)
        upper_tiles = upper.reshape(2 * edge, col_tiles, edge).transpose(1, 0, 2)
        left = lower_tiles[local_row]
        right = upper_tiles[local_col]
        product = jnp.einsum("sik,skj->sij", left, right, preferred_element_type=jnp.float32)
        updated = (current.astype(jnp.float32) - product).astype(jnp.bfloat16)
        lower_parts = lower_tiles.reshape(row_tiles, edge, 2, edge).transpose(0, 2, 1, 3)
        lower_write = lower_parts[local_row, jnp.clip(tile_col - first, 0, 1)]
        upper_parts = upper_tiles.reshape(col_tiles, 2, edge, edge)
        upper_write = upper_parts[local_col, jnp.clip(tile_row - first, 0, 1)]
        trailing = (tile_row >= first + 2) & (tile_col >= first + 2)
        is_lower = in_column & (tile_row >= first + 2)
        current = jnp.where(trailing[:, None, None], updated, current)
        current = jnp.where(is_lower[:, None, None], lower_write, current)
        current = jnp.where(in_block[:, None, None], upper_write, current)
    return current


def solution(mesh):
    return jax.shard_map(
        local,
        mesh=mesh,
        in_specs=(P(("prow", "pcol"), None, None), P(("prow", "pcol"), None), P(), P()),
        out_specs=P(("prow", "pcol"), None, None),
        check_vma=False,
    )
```

profile of v0, /device:TPU:1, one launch (start us, length us, event | category | flops | bytes accessed | tf_op | source)
XLA Modules:
  0.0 537.5 jit_solution(18304019834849628285)
XLA Ops:
  6.5 0.8 add_select_fusion
  7.3 0.8 broadcast_select_fusion.4
  8.3 2.9 gather_fusion
  11.5 0.7 copy.34
  12.2 1.3 copy.35
  13.5 0.7 copy.36
  14.2 1.3 copy.37
  15.8 4.3 gather_fusion.3
  20.3 1.8 select_bitcast_fusion.1
  22.1 2.9 conditional.2
  22.1 2.2 copy.39
  24.3 0.7 convolution_convert_fusion
  25.0 1.4 broadcast_select_fusion.1
  26.6 0.6 copy-done.3
  27.9 106.4 %all-reduce.13.cloned.1.call-done = (bf16[128,4096]{1,0:T(8,128)(2,1)}, bf16[128,4096]{1,0:T(8,128)(2,1)}) async-done(((bf16[128,4096]{1,0:T(8,128)(2,1)}, bf16[128,4096]{1,0:T(8,128)(2,1)}), (bf16[128,4096]{1,0:T(8,128)(2,1)}, bf16[128,4096]{1,0:T(8,128)(2,1)})) %all-reduce.13.cloned.1.call-update) | async-done | bytes 2097168 | tf_op jit(solution)/shard_map/psum | solution.py:11
  134.3 1.7 pad_maximum_fusion
  136.0 3.2 gather_fusion.1
  139.2 4.0 fusion.42
  143.1 4.7 gather_fusion.2
  147.9 6.8 %gather_fusion.6 = bf16[128,256,128]{2,1,0:T(8,128)(2,1)} fusion(bf16[32,256,128]{2,1,0:T(8,128)(2,1)S(1)} %get-tuple-element.55, s32[1024]{0:T(1024)S(1)} %pad_clamp_fusion.3), kind=kCustom, calls=%fused_computation.6 | custom fusion | bytes 16777728 | tf_op jit(solution)/shard_map/gather | solution.py:69
  154.6 82.7 %all-reduce.7.cloned.1.call-done = bf16[4096,256]{1,0:T(8,128)(2,1)} async-done(((bf16[4096,256]{1,0:T(8,128)(2,1)}), bf16[4096,256]{1,0:T(8,128)(2,1)}) %all-reduce.7.cloned.1.call-update) | async-done | bytes 2097168 | tf_op jit(solution)/shard_map/psum | solution.py:11
  237.3 2.5 reshape.507
  239.9 1.8 copy.75
  241.7 4.8 gather_fusion.4
  246.5 6.6 %gather_fusion.5 = bf16[128,128,256]{2,1,0:T(8,128)(2,1)} fusion(bf16[32,128,256]{2,1,0:T(8,128)(2,1)S(1)} %bitcast.156, s32[1024]{0:T(1024)S(1)} %pad_clamp_fusion.4), kind=kCustom, calls=%fused_computation.5 | custom fusion | bytes 16777728 | tf_op jit(solution)/shard_map/gather | solution.py:68
  253.1 16.2 %fusion.13 = bf16[128,128,128]{2,1,0:T(8,128)(2,1)} fusion(bf16[128,128,128]{2,1,0:T(8,128)(2,1)} %gather_fusion.2, bf16[128,128,128]{2,1,0:T(8,128)(2,1)} %gather_fusion.4, bf16[128,128,128]{2,1,0:T(8,128)(2,1)} %param.8, pred[128]{0:T(512)(128)(4,1)S(1)} %get-tuple-element.67, pred[128]{0:T(512)(128)(4,1)S(1)} %get-tuple-element.68, ...), kind=kOutput, calls=%fused_computation.31 | convolution fusion | flops 1086324736 | bytes 33554816 | tf_op jit(solution)/shard_map/sik,skj->sij/dot_general | solution.py:70
  269.3 2.9 gather_fusion.7
  272.3 0.2 select_bitcast_fusion.3
  272.5 0.7 copy.42
  273.1 1.3 copy.43
  274.5 0.7 copy.44
  275.1 1.3 copy.45
  276.5 4.4 gather_fusion.10
  280.9 1.8 select_bitcast_fusion
  282.7 0.4 conditional.3
  283.1 1.5 broadcast_select_fusion
  284.7 111.5 %all-reduce.11.cloned.1.call-done = (bf16[128,4096]{1,0:T(8,128)(2,1)}, bf16[128,4096]{1,0:T(8,128)(2,1)}) async-done(((bf16[128,4096]{1,0:T(8,128)(2,1)}, bf16[128,4096]{1,0:T(8,128)(2,1)}), (bf16[128,4096]{1,0:T(8,128)(2,1)}, bf16[128,4096]{1,0:T(8,128)(2,1)})) %all-reduce.11.cloned.1.call-update) | async-done | bytes 2097168 | tf_op jit(solution)/shard_map/psum | solution.py:11
  396.2 1.7 pad_maximum_fusion.1
  397.8 3.2 gather_fusion.8
  401.0 3.9 fusion.43
  405.0 6.7 %gather_fusion.13 = bf16[128,256,128]{2,1,0:T(8,128)(2,1)} fusion(bf16[32,256,128]{2,1,0:T(8,128)(2,1)S(1)} %get-tuple-element.53, s32[1024]{0:T(1024)S(1)} %pad_clamp_fusion.3), kind=kCustom, calls=%fused_computation.13 | custom fusion | bytes 16777728 | tf_op jit(solution)/shard_map/gather | solution.py:69
  411.6 4.6 gather_fusion.9
  416.3 83.2 %all-reduce.9.cloned.1.call-done = bf16[4096,256]{1,0:T(8,128)(2,1)} async-done(((bf16[4096,256]{1,0:T(8,128)(2,1)}), bf16[4096,256]{1,0:T(8,128)(2,1)}) %all-reduce.9.cloned.1.call-update) | async-done | bytes 2097168 | tf_op jit(solution)/shard_map/psum | solution.py:11
  499.5 8.3 %gather_fusion.12 = bf16[128,128,256]{2,1,0:T(8,128)(2,1)} fusion(bf16[32,128,256]{2,1,0:T(8,128)(2,1)} %bitcast.157, s32[1024]{0:T(1024)S(1)} %pad_clamp_fusion.4), kind=kCustom, calls=%fused_computation.12 | custom fusion | bytes 16777728 | tf_op jit(solution)/shard_map/gather | solution.py:68
  507.8 2.1 reshape.508
  509.8 2.1 copy.74
  512.0 3.1 gather_fusion.11
  515.1 15.9 %fusion.11 = bf16[128,128,128]{2,1,0:T(8,128)(2,1)} fusion(bf16[128,128,128]{2,1,0:T(8,128)(2,1)} %gather_fusion.9, bf16[128,128,128]{2,1,0:T(8,128)(2,1)} %gather_fusion.11, bf16[128,128,128]{2,1,0:T(8,128)(2,1)} %fusion.13, pred[128]{0:T(512)(128)(4,1)S(1)} %get-tuple-element.66, pred[128]{0:T(512)(128)(4,1)S(1)} %get-tuple-element.64, ...), kind=kOutput, calls=%fused_computation.29 | convolution fusion | flops 1086324736 | bytes 33554816 | tf_op jit(solution)/shard_map/sik,skj->sij/dot_general | solution.py:70
  (45 shorter events, 1.8 us)
Async XLA Ops:
  6.5 127.8 %all-reduce.13.cloned.1.call-start = ((), (), s32[]{:S(2)}) async-start(), calls=%async_computation.3 | async-start | bytes 4194304 | tf_op jit(solution)/shard_map/psum | solution.py:11
  15.5 221.8 %all-reduce.7.cloned.1.call-start = ((), (), s32[]{:S(2)}) async-start(), calls=%async_computation | async-start | bytes 4194304 | tf_op jit(solution)/shard_map/psum | solution.py:11
  20.3 1.9 copy-start.2
  26.5 0.7 copy-start.3
  26.5 0.7 copy-start.4
  26.5 369.7 %all-reduce.11.cloned.1.call-start = ((), (), s32[]{:S(2)}) async-start(), calls=%async_computation.2 | async-start | bytes 4194304 | tf_op jit(solution)/shard_map/psum | solution.py:11
  241.7 4.8 copy-start
  280.8 218.6 %all-reduce.9.cloned.1.call-start = ((), (), s32[]{:S(2)}) async-start(), calls=%async_computation.1 | async-start | bytes 4194304 | tf_op jit(solution)/shard_map/psum | solution.py:11
  499.5 8.3 %copy-start.1 = (bf16[4096,256]{1,0:T(8,128)(2,1)S(1)}, bf16[4096,256]{1,0:T(8,128)(2,1)}, u32[]{:S(2)}) copy-start(bf16[4096,256]{1,0:T(8,128)(2,1)} %all-reduce.9.cloned.1.call-done) | copy-start | bytes 6291460
Sparse Core Ops, SparseCore 0:
  15.6 118.6 all-reduce.12
  137.6 99.6 all-reduce.6
  281.0 115.1 all-reduce.10
  399.7 99.7 all-reduce.8
where the time goes:
time: 538 us
  waiting for transfers between devices  384 us (71%)
  local copies, waits for them, and re-layouts  94.1 us (17%)
  matrix products  32.9 us (6%)
  between operations  13.5 us (3%)
  other arithmetic  12.9 us (2%)
    psum x4, waiting for transfers between devices, broadcast(): return lax.psum(jnp.where(mine, value, jnp.zeros_like(value)), axis)  384 us
    dot_general x2, matrix products, local(): jnp.einsum('sik,skj->sij', left, right, preferred_element_type=jnp.float32)  32.2 us
    gather x2, local copies, waits for them, and re-layouts, local(): left = lower_tiles[local_row]  14.9 us
    gather x2, local copies, waits for them, and re-layouts, local(): right = upper_tiles[local_col]  13.5 us
  transfers between devices with their start and end apart: 4, of which 4 were waited for; matrix products, arithmetic and copies ran while one was open for 10% of the time, Pallas kernels for 0%

commit v1 on v0

v1 whole, which is shorter than its diff:
```python
import functools

import jax
import jax.numpy as jnp
from jax import lax
from jax.experimental import pallas as pl
from jax.experimental.pallas import tpu as pltpu
from jax.sharding import PartitionSpec as P

T = 128
BF = jnp.bfloat16
F32 = jnp.float32
SLOTS = 128
ROWS = 32
COLS = 32


ALONG_Y = [[x * 4 + y for y in range(4)] for x in range(4)]
SAME_CORE = [[z * 2 + c for z in range(8)] for c in range(2)]
SWAP = [(p, p ^ 1) for p in range(16)]
UP_Z = [(p, (p + 2) % 16) for p in range(16)]


def move_x(d):
    return [(x * 4 + y, (x + d) % 4 * 4 + y) for x in range(4) for y in range(4)]


def move_y(d):
    return [(x * 4 + y, x * 4 + (y + d) % 4) for x in range(4) for y in range(4)]


def scatter_z(m):
    return [(k * 2 + c, (2 * m + k) * 2 + c) for k in range(2) for c in range(2)]


VM = pl.BlockSpec(memory_space=pltpu.VMEM)
SM = pl.BlockSpec(memory_space=pltpu.SMEM)


def extract_columns_kernel(pos, tiles, col):
    @pl.loop(0, SLOTS)
    def _(s):
        i = pos[0, s]
        j = pos[1, s]

        @pl.when((j >= 0) & (j < 4))
        def _():
            col[(i // 16) * 2 + j % 2] = tiles[s]


def extract_rows_kernel(pos, tiles, after, *quarters):
    @pl.loop(0, SLOTS)
    def _(s):
        i = pos[0, s]
        j = pos[1, s]

        @pl.when((i >= 0) & (i < 4))
        def _():
            lj = (j // 32) * 2 + j % 2
            for m in range(4):
                @pl.when(lj // 8 == m)
                def _():
                    quarters[m][lj % 8] = tiles[s]

            @pl.when(lj < 2)
            def _():
                for m in range(4):
                    quarters[m][8 + lj] = tiles[s]


def extract_columns(pos_t, tiles):
    return pl.pallas_call(
        extract_columns_kernel,
        out_shape=jax.ShapeDtypeStruct((2 * ROWS, T, T), BF),
        in_specs=[SM, VM],
        out_specs=VM,
        compiler_params=pltpu.CompilerParams(vmem_limit_bytes=16 << 20),
        name="extract_columns",
    )(pos_t, tiles)


def extract_rows(pos_t, tiles, after):
    return pl.pallas_call(
        extract_rows_kernel,
        out_shape=[jax.ShapeDtypeStruct((COLS // 4 + 2, T, T), BF)] * 4,
        in_specs=[SM, VM, pl.BlockSpec(memory_space=pl.ANY)],
        out_specs=[VM] * 4,
        compiler_params=pltpu.CompilerParams(vmem_limit_bytes=16 << 20),
        name="extract_rows",
    )(pos_t, tiles, after)


def dot(a, b):
    return jnp.dot(a, b, preferred_element_type=F32)


def update_kernel(
    pos, me, tiles, pivots, inverses, panel0, b0, b1, b2, b3, rows_mine, rows_other, corner_other,
    out, lc, uc,
):
    p, q = me[0], me[1]
    c = p % 2
    my_x, my_y = q // 4, q % 4
    w0 = inverses[0]
    w1 = inverses[1]

    place = lax.broadcasted_iota(jnp.int32, (256, 256), 0)
    place = jnp.where(place < 128, place + c * 128, place - c * 128)

    def permutation(k):
        hot = (jnp.broadcast_to(pivots[k : k + 1, :], (256, 256)) == place).astype(F32)
        return hot.T.astype(BF)

    perm0 = permutation(0)
    perm1 = permutation(1)

    def pair(mine, m, other, o):
        top = jnp.concatenate([mine[m], mine[m + 1]], axis=1)
        low = jnp.concatenate([other[o], other[o + 1]], axis=1)
        return jnp.concatenate([top, low], axis=0)

    low_rows = dot(pair(panel0, 16, corner_other, 0), w0).astype(BF)
    corner = dot(perm0, pair(panel0, 34, corner_other, 2)).astype(BF)

    @pl.loop(0, 4)
    def _(m):
        def rows(base):
            return jnp.concatenate(
                [pair(rows_mine, base + 2 * h, rows_other, base + 2 * h) for h in range(4)], axis=1
            )

        first = dot(perm0, rows(m * 16)).astype(BF)
        new = (rows(m * 16 + 8).astype(F32) - dot(low_rows, first)).astype(BF)
        head = jnp.where((m == 0) & (q == 0), low_rows, new[:, :256])
        second = dot(perm1, jnp.concatenate([head, new[:, 256:]], axis=1)).astype(BF)
        for t in range(8):
            uc[8 * m + t, :256] = first[:, 128 * t : 128 * t + 128]
            uc[8 * m + t, 256:] = second[:, 128 * t : 128 * t + 128]

    def blocks(ref, base):
        rows = [
            jnp.concatenate([ref[base + 2 * g], ref[base + 2 * g + 1]], axis=1) for g in range(8)
        ]
        return jnp.concatenate(rows, axis=0)

    shifts = (0, 3, 1, 2)

    @pl.loop(0, 4)
    def _(y):
        low = dot(blocks(panel0, y * 18), w0).astype(BF)
        for g, dx in enumerate(shifts):
            row = 2 * ((my_x + dx) % 4 * 4 + y)
            lc[row, :, :256] = low[g * 256 : g * 256 + 128]
            lc[row + 1, :, :256] = low[g * 256 + 128 : g * 256 + 256]

    for ref, dx in zip((b0, b1, b2, b3), shifts):
        row_of = [2 * ((my_x + dx) % 4 * 4 + (my_y + dy) % 4) for dy in shifts]
        left = jnp.concatenate([lc[r + h, :, :256] for r in row_of for h in range(2)], axis=0)
        new = (blocks(ref, 0).astype(F32) - dot(left, corner)).astype(BF)
        low = dot(new, w1).astype(BF)
        for g, r in enumerate(row_of):
            lc[r, :, 256:] = low[g * 256 : g * 256 + 128]
            lc[r + 1, :, 256:] = low[g * 256 + 128 : g * 256 + 256]

    def place_of(s):
        i = pos[0, s]
        j = pos[1, s]
        li = jnp.clip(i // 16, 0, ROWS - 1)
        lj = jnp.clip((j // 32) * 2 + j % 2, 0, COLS - 1)
        return i, j, li, lj

    def finish(s):
        i, j, li, lj = place_of(s)

        @pl.when(i < 0)
        def _():
            out[s] = tiles[s]

        @pl.when((i >= 0) & (i < 4))
        def _():
            start = pl.multiple_of((i // 2) * 256 + c * 128, 128)
            out[s] = uc[lj, pl.ds(start, 128), :]

        for t in range(4):
            @pl.when((i >= 4) & (j == t))
            def _():
                out[s] = lc[li, :, t * 128 : t * 128 + 128]

    @pl.loop(0, SLOTS // 8)
    def _(b):
        least = jnp.int32(4)
        for k in range(8):
            s = b * 8 + k
            i, j, li, lj = place_of(s)
            least = jnp.minimum(least, jnp.minimum(i, j))
            out[s] = (tiles[s].astype(F32) - dot(lc[li], uc[lj])).astype(BF)

        @pl.when(least < 4)
        def _():
            @pl.loop(b * 8, b * 8 + 8)
            def _(s):
                finish(s)


def update(*args):
    return pl.pallas_call(
        update_kernel,
        out_shape=jax.ShapeDtypeStruct((SLOTS, T, T), BF),
        in_specs=[SM, SM] + [VM] * (len(args) - 2),
        out_specs=VM,
        scratch_shapes=[
            pltpu.VMEM((ROWS, T, 4 * T), BF),
            pltpu.VMEM((COLS, 4 * T, T), BF),
        ],
        compiler_params=pltpu.CompilerParams(vmem_limit_bytes=48 << 20),
        name="update",
    )(*args)


def spread(piece, groups):
    copies = jnp.broadcast_to(piece[None], (4,) + piece.shape).reshape(-1, T, T)
    return lax.all_to_all(copies, "pcol", 0, 0, tiled=True, axis_index_groups=groups)


def around(piece, move):
    return [piece] + [lax.ppermute(piece, "pcol", move(d)) for d in (1, -1, 2)]


def local(tiles, tile_pos, pivots, inverses):
    p = lax.axis_index("prow")
    q = lax.axis_index("pcol")
    pos_t = tile_pos.T
    me = jnp.stack([p, q]).astype(jnp.int32)
    col = extract_columns(pos_t, tiles)
    quarters = extract_rows(pos_t, tiles, col)

    with jax.named_scope("row_scatter"):
        quarter = quarters[0]
        for m in range(1, 4):
            got = lax.ppermute(quarters[m], "prow", scatter_z(m))
            quarter = jnp.where(p // 4 == m, got, quarter)
    with jax.named_scope("column_scatter"):
        shards = lax.all_to_all(col, "pcol", 0, 0, tiled=True)
    with jax.named_scope("row_gather"):
        rows_mine = lax.all_gather(
            quarter[:8], "prow", tiled=True, axis_index_groups=SAME_CORE
        )
    with jax.named_scope("corner_gather"):
        held, shards = lax.optimization_barrier((quarter[8:], shards))
        below = lax.ppermute(held, "prow", UP_Z)
        corner = jnp.where((p // 2 + q) % 2 == 1, held, below)
    with jax.named_scope("column_gather"):
        first0 = around(jnp.concatenate([shards[:4], corner]), move_x)
        first1 = jnp.concatenate(around(shards[4:8], move_y))
        x = q // 4
        corner = first0[0][4:]
        for k, g in ((1, 1), (2, 3), (3, 2)):
            corner = jnp.where(x == k, first0[g][4:], corner)
        join0 = [g[:4] for g in first0] + [corner]
        panel0 = spread(jnp.concatenate(join0), ALONG_Y)
        panel1 = around(first1, move_x)
    with jax.named_scope("core_swap"):
        late, _ = lax.optimization_barrier((rows_mine, first1))
        rows_other = lax.ppermute(late, "prow", SWAP)
        corner_other = lax.ppermute(jnp.concatenate([panel0[16:18], panel0[34:36]]), "prow", SWAP)
    return update(
        pos_t, me, tiles, pivots, inverses, panel0, *panel1, rows_mine, rows_other, corner_other
    )


def solution(mesh):
    return jax.shard_map(
        local,
        mesh=mesh,
        in_specs=(P(("prow", "pcol"), None, None), P(("prow", "pcol"), None), P(), P()),
        out_specs=P(("prow", "pcol"), None, None),
        check_vma=False,
    )
```

time: 538 us -> 159 us (0.30)
  waiting for transfers between devices: 384 us -> 48.8 us
  local copies, waits for them, and re-layouts: 94.1 us -> 8.17 us
  starting transfers between devices: 0.13 us -> 53.6 us
  Pallas kernels: 0 us -> 34.4 us
  matrix products: 32.9 us -> 0 us
  other arithmetic: 12.9 us -> 0.33 us
    psum x4 -> x0, waiting for transfers between devices: 384 us -> none  [broadcast(): return lax.psum(jnp.where(mine, value, jnp.zeros_like(value)), axis)]
    gather x14 -> x0, local copies, waits for them, and re-layouts: 66.5 us -> none  [the longest x2 14.9 us: local(): left = lower_tiles[local_row]]
    ppermute x0 -> x15, starting transfers between devices: none -> 42.6 us  [the longest x3 12.5 us: local(): got = lax.ppermute(quarters[m], 'prow', scatter_z(m))]
    pallas_call x0 -> x3, Pallas kernels: none -> 34.4 us  [the longest x1 26.3 us: update(): pl.pallas_call(update_kernel, out_shape=jax.ShapeDtypeStruct((SLOTS, T, T...]
    dot_general x3 -> x0, matrix products: 32.9 us -> none  [the longest x2 32.2 us: local(): jnp.einsum('sik,skj->sij', left, right, preferred_element_type=jnp.float32)]
    all_to_all x0 -> x2, waiting for transfers between devices: none -> 24.2 us  [the longest x1 15.5 us: local(): shards = lax.all_to_all(col, 'pcol', 0, 0, tiled=True)]
    ppermute x0 -> x15, waiting for transfers between devices: none -> 24 us  [the longest x3 9.6 us: local(): got = lax.ppermute(quarters[m], 'prow', scatter_z(m))]
    all_to_all x0 -> x2, starting transfers between devices: none -> 10.9 us  [the longest x1 6.28 us: local(): shards = lax.all_to_all(col, 'pcol', 0, 0, tiled=True)]
  transfers between devices with their start and end apart: 4 -> 18, of which waited for: 4 -> 9; matrix products, arithmetic and copies ran while one was open for 10% -> 3% of each run, Pallas kernels for 0% -> 0%
where the time goes in v1:
time: 159 us
  starting transfers between devices  53.6 us (34%)
  waiting for transfers between devices  48.8 us (31%)
  Pallas kernels  34.4 us (22%)
  between operations  13.6 us (9%)
  local copies, waits for them, and re-layouts  8.17 us (5%)
    pallas_call x1, Pallas kernels, update(): pl.pallas_call(update_kernel, out_shape=jax.ShapeDtypeStruct((SLOTS, T, T...  26.3 us
    all_to_all x1, waiting for transfers between devices, local(): shards = lax.all_to_all(col, 'pcol', 0, 0, tiled=True)  15.5 us
    ppermute x3, starting transfers between devices, local(): got = lax.ppermute(quarters[m], 'prow', scatter_z(m))  12.5 us
    ppermute x1, starting transfers between devices, local(): lax.ppermute(jnp.concatenate([panel0[16:18], panel0[34:36]]), 'prow', SWAP)  10.6 us
    ppermute x9, starting transfers between devices, around(): return [piece] + [lax.ppermute(piece, 'pcol', move(d)) for d in (1, -1, 2)]  10 us
    ppermute x3, waiting for transfers between devices, local(): got = lax.ppermute(quarters[m], 'prow', scatter_z(m))  9.6 us
    ppermute x9, waiting for transfers between devices, around(): return [piece] + [lax.ppermute(piece, 'pcol', move(d)) for d in (1, -1, 2)]  9.34 us
    ppermute x1, starting transfers between devices, local(): rows_other = lax.ppermute(late, 'prow', SWAP)  8.82 us
  transfers between devices with their start and end apart: 18, of which 9 were waited for; matrix products, arithmetic and copies ran while one was open for 3% of the time, Pallas kernels for 0%

profile of v1, /device:TPU:1, one launch (start us, length us, event | category | flops | bytes accessed | tf_op | source)
XLA Modules:
  0.0 158.9 jit_solution(3093948785740746477)
XLA Ops:
  6.5 2.2 %copy-done = bf16[128,128,128]{2,1,0:T(8,128)(2,1)S(1)} copy-done((bf16[128,128,128]{2,1,0:T(8,128)(2,1)S(1)}, bf16[128,128,128]{2,1,0:T(8,128)(2,1)}, u32[]{:S(2)}) %copy-start) | copy-done | bytes 4194328
  8.7 0.7 copy-done.3
  9.4 4.5 %extract_columns.1.after = bf16[64,128,128]{2,1,0:T(8,128)(2,1)} custom-call(s32[2,128]{1,0:T(2,128)S(1)} %bitcast.4, bf16[128,128,128]{2,1,0:T(8,128)(2,1)S(1)} %copy-done), custom_call_target="tpu_custom_call" | custom-call | tf_op jit(solution)/shard_map/extract_columns/pallas_call | solution.py:72
  13.9 3.6 %extract_rows.1 = (bf16[10,128,128]{2,1,0:T(8,128)(2,1)S(1)}, bf16[10,128,128]{2,1,0:T(8,128)(2,1)S(1)}, bf16[10,128,128]{2,1,0:T(8,128)(2,1)S(1)}, bf16[10,128,128]{2,1,0:T(8,128)(2,1)S(1)}) custom-call(s32[2,128]{1,0:T(2,128)S(1)} %bitcast.5, bf16[128,128,128]{2,1,0:T(8,128)(2,1)S(1)} %copy-done, bf16[64,128,128]{2,1,0:T(8,128)(2,1)} %extract_columns.1.after), custom_call_target="tpu_custom_call" | custom-call | tf_op jit(solution)/shard_map/extract_rows/pallas_call | solution.py:83
  17.5 8.2 %collective-permute-start = (bf16[10,128,128]{2,1,0:T(8,128)(2,1)S(1)}, bf16[10,128,128]{2,1,0:T(8,128)(2,1)}, u32[]{:S(2)}, u32[]{:S(2)}) collective-permute-start(bf16[10,128,128]{2,1,0:T(8,128)(2,1)S(1)} %get-tuple-element.12), channel_id=1, source_target_pairs={{0,192},{16,208},{32,224},{48,240},{1,193},{17,209},{33,225},{49,2... | collective-permute-start | bytes 983048 | tf_op jit(solution)/shard_map/row_scatter/ppermute | solution.py:240
  25.7 2.3 %collective-permute-start.1 = (bf16[10,128,128]{2,1,0:T(8,128)(2,1)S(1)}, bf16[10,128,128]{2,1,0:T(8,128)(2,1)}, u32[]{:S(2)}, u32[]{:S(2)}) collective-permute-start(bf16[10,128,128]{2,1,0:T(8,128)(2,1)S(1)} %get-tuple-element.13), channel_id=1, source_target_pairs={{0,128},{16,144},{32,160},{48,176},{1,129},{17,145},{33,161},{49,1... | collective-permute-start | bytes 983048 | tf_op jit(solution)/shard_map/row_scatter/ppermute | solution.py:240
  28.0 2.0 %collective-permute-start.2 = (bf16[10,128,128]{2,1,0:T(8,128)(2,1)S(1)}, bf16[10,128,128]{2,1,0:T(8,128)(2,1)}, u32[]{:S(2)}, u32[]{:S(2)}) collective-permute-start(bf16[10,128,128]{2,1,0:T(8,128)(2,1)S(1)} %get-tuple-element.14), channel_id=1, source_target_pairs={{0,64},{16,80},{32,96},{48,112},{1,65},{17,81},{33,97},{49,113},{2... | collective-permute-start | bytes 983048 | tf_op jit(solution)/shard_map/row_scatter/ppermute | solution.py:240
  30.0 6.3 %all-to-all-start = ((bf16[64,128,128]{2,1,0:T(8,128)(2,1)}), bf16[64,128,128]{2,1,0:T(8,128)(2,1)S(1)}, u32[]{:S(2)}, u32[]{:S(2)}) async-start(bf16[64,128,128]{2,1,0:T(8,128)(2,1)} %extract_columns.1.after), calls=%async_computation | async-start | bytes 4194304 | tf_op jit(solution)/shard_map/column_scatter/all_to_all | solution.py:243
  36.3 0.0 all-gather.2.cloned.1.call-start
  36.4 9.6 %collective-permute-done = bf16[10,128,128]{2,1,0:T(8,128)(2,1)} collective-permute-done((bf16[10,128,128]{2,1,0:T(8,128)(2,1)S(1)}, bf16[10,128,128]{2,1,0:T(8,128)(2,1)}, u32[]{:S(2)}, u32[]{:S(2)}) %collective-permute-start) | collective-permute-done | bytes 327712 | tf_op jit(solution)/shard_map/row_scatter/ppermute | solution.py:240
  46.0 0.0 collective-permute-done.1
  46.0 0.0 collective-permute-done.2
  46.0 0.1 select_select_fusion
  46.0 0.7 slice.55
  46.8 0.0 all-gather.2.cloned.1.call-update
  46.9 15.5 %all-to-all-done = bf16[64,128,128]{2,1,0:T(8,128)(2,1)S(1)} async-done(((bf16[64,128,128]{2,1,0:T(8,128)(2,1)}), bf16[64,128,128]{2,1,0:T(8,128)(2,1)S(1)}, u32[]{:S(2)}, u32[]{:S(2)}) %all-to-all-start) | async-done | bytes 2097184 | tf_op jit(solution)/shard_map/column_scatter/all_to_all | solution.py:243
  62.4 0.7 collective-permute-start.3
  63.2 5.0 %collective-permute-done.3 = bf16[2,128,128]{2,1,0:T(8,128)(2,1)S(1)} collective-permute-done((bf16[2,128,128]{2,1,0:T(8,128)(2,1)S(1)}, bf16[2,128,128]{2,1,0:T(8,128)(2,1)S(1)}, u32[]{:S(2)}, u32[]{:S(2)}) %collective-permute-start.3) | collective-permute-done | bytes 65568 | tf_op jit(solution)/shard_map/corner_gather/ppermute | solution.py:250
  68.3 0.3 collective-permute-start.4
  68.5 3.7 %collective-permute-start.9 = (bf16[4,128,128]{2,1,0:T(8,128)(2,1)S(1)}, bf16[4,128,128]{2,1,0:T(8,128)(2,1)S(1)}, u32[]{:S(2)}, u32[]{:S(2)}) collective-permute-start(bf16[4,128,128]{2,1,0:T(8,128)(2,1)S(1)} %get-tuple-element.21), channel_id=1, source_target_pairs={{0,2},{1,3},{2,0},{3,1},{4,6},{5,7},{6,4},{7,5},{8,10},{9,11},{10,... | collective-permute-start | bytes 393224 | tf_op jit(solution)/shard_map/column_gather/ppermute | solution.py:226
  72.2 0.0 collective-permute-start.8
  72.2 1.5 collective-permute-start.7
  73.7 0.9 collective-permute-start.6
  74.6 0.0 collective-permute-done.4
  74.6 2.0 %collective-permute-start.5 = (bf16[6,128,128]{2,1,0:T(8,128)(2,1)S(1)}, bf16[6,128,128]{2,1,0:T(8,128)(2,1)S(1)}, u32[]{:S(2)}, u32[]{:S(2)}) collective-permute-start(bf16[6,128,128]{2,1,0:T(8,128)(2,1)S(1)} %pad_maximum_fusion.1), channel_id=1, source_target_pairs={{0,12},{1,13},{2,14},{3,15},{4,0},{5,1},{6,2},{7,3},{8,4},{9,5},{1... | collective-permute-start | bytes 589832 | tf_op jit(solution)/shard_map/column_gather/ppermute | solution.py:226
  76.6 4.0 %collective-permute-done.5 = bf16[6,128,128]{2,1,0:T(8,128)(2,1)S(1)} collective-permute-done((bf16[6,128,128]{2,1,0:T(8,128)(2,1)S(1)}, bf16[6,128,128]{2,1,0:T(8,128)(2,1)S(1)}, u32[]{:S(2)}, u32[]{:S(2)}) %collective-permute-start.5) | collective-permute-done | bytes 196640 | tf_op jit(solution)/shard_map/column_gather/ppermute | solution.py:226
  80.7 0.6 collective-permute-done.6
  81.3 0.1 fusion.2
  81.3 2.0 %broadcast_in_dim.2 = bf16[4,18,128,128]{3,2,1,0:T(8,128)(2,1)} broadcast(bf16[18,128,128]{2,1,0:T(8,128)(2,1)S(1)} %fusion.2), dimensions={1,2,3} | broadcast | bytes 2949120 | tf_op jit(solution)/shard_map/column_gather/broadcast_in_dim | solution.py:221
  83.3 4.6 %all-to-all-start.1 = ((bf16[72,128,128]{2,1,0:T(8,128)(2,1)}), bf16[72,128,128]{2,1,0:T(8,128)(2,1)}, u32[]{:S(2)}, u32[]{:S(2)}) async-start(bf16[72,128,128]{2,1,0:T(8,128)(2,1)} %bitcast.3), calls=%async_computation.1 | async-start | bytes 4718592 | tf_op jit(solution)/shard_map/column_gather/all_to_all | solution.py:222
  88.0 0.0 collective-permute-done.9
  88.0 0.0 collective-permute-done.8
  88.0 0.0 collective-permute-done.7
  88.0 0.1 pad_maximum_fusion.b0
  88.1 0.6 all-gather.2.cloned.1.call-done.rows_mine
  88.7 8.8 %collective-permute-start.13 = (bf16[64,128,128]{2,1,0:T(8,128)(2,1)}, bf16[64,128,128]{2,1,0:T(8,128)(2,1)}, u32[]{:S(2)}, u32[]{:S(2)}) collective-permute-start(bf16[64,128,128]{2,1,0:T(8,128)(2,1)} %all-gather.2.cloned.1.call-done.rows_mine), channel_id=1, source_target_pairs={{0,16},{16,0},{32,48},{48,32},{64,80},{80,64},{96,112},{112,96},{1... | collective-permute-start | bytes 6291464 | tf_op jit(solution)/shard_map/core_swap/ppermute | solution.py:264
  97.5 0.0 collective-permute-start.12
  97.5 1.7 %collective-permute-start.11 = (bf16[16,128,128]{2,1,0:T(8,128)(2,1)S(1)}, bf16[16,128,128]{2,1,0:T(8,128)(2,1)S(1)}, u32[]{:S(2)}, u32[]{:S(2)}) collective-permute-start(bf16[16,128,128]{2,1,0:T(8,128)(2,1)S(1)} %pad_maximum_fusion.b0), channel_id=1, source_target_pairs={{0,12},{1,13},{2,14},{3,15},{4,0},{5,1},{6,2},{7,3},{8,4},{9,5},{1... | collective-permute-start | bytes 1572872 | tf_op jit(solution)/shard_map/column_gather/ppermute | solution.py:226
  99.2 8.6 %all-to-all-done.1.panel0 = bf16[72,128,128]{2,1,0:T(8,128)(2,1)} async-done(((bf16[72,128,128]{2,1,0:T(8,128)(2,1)}), bf16[72,128,128]{2,1,0:T(8,128)(2,1)}, u32[]{:S(2)}, u32[]{:S(2)}) %all-to-all-start.1) | async-done | bytes 2359328 | tf_op jit(solution)/shard_map/column_gather/all_to_all | solution.py:222
  107.8 0.9 fusion.3
  108.7 10.6 %collective-permute-start.14 = (bf16[4,128,128]{2,1,0:T(8,128)(2,1)S(1)}, bf16[4,128,128]{2,1,0:T(8,128)(2,1)S(1)}, u32[]{:S(2)}, u32[]{:S(2)}) collective-permute-start(bf16[4,128,128]{2,1,0:T(8,128)(2,1)S(1)} %pad_maximum_fusion.2), channel_id=1, source_target_pairs={{0,16},{16,0},{32,48},{48,32},{64,80},{80,64},{96,112},{112,96},{1... | collective-permute-start | bytes 393224 | tf_op jit(solution)/shard_map/core_swap/ppermute | solution.py:265
  119.3 0.1 pad_add_fusion.me
  119.4 0.0 collective-permute-done.12.b3
  119.4 2.9 %collective-permute-done.11.b2 = bf16[16,128,128]{2,1,0:T(8,128)(2,1)S(1)} collective-permute-done((bf16[16,128,128]{2,1,0:T(8,128)(2,1)S(1)}, bf16[16,128,128]{2,1,0:T(8,128)(2,1)S(1)}, u32[]{:S(2)}, u32[]{:S(2)}) %collective-permute-start.11) | collective-permute-done | bytes 524320 | tf_op jit(solution)/shard_map/column_gather/ppermute | solution.py:226
  122.3 1.8 %collective-permute-done.10.b1 = bf16[16,128,128]{2,1,0:T(8,128)(2,1)S(1)} collective-permute-done((bf16[16,128,128]{2,1,0:T(8,128)(2,1)S(1)}, bf16[16,128,128]{2,1,0:T(8,128)(2,1)S(1)}, u32[]{:S(2)}, u32[]{:S(2)}) %collective-permute-start.10) | collective-permute-done | bytes 524320 | tf_op jit(solution)/shard_map/column_gather/ppermute | solution.py:226
  124.1 0.0 collective-permute-done.14.corner_other
  124.1 1.6 copy-done.1
  125.7 26.3 %update.1 = bf16[128,128,128]{2,1,0:T(8,128)(2,1)} custom-call(s32[2,128]{1,0:T(2,128)S(1)} %bitcast.6, s32[2]{0:T(128)S(1)} %pad_add_fusion.me, bf16[128,128,128]{2,1,0:T(8,128)(2,1)} %tiles.5, s32[2,256]{1,0:T(2,128)S(1)} %copy-done.5, bf16[2,256,256]{2,1,0:T(8,128)(2,1)S(1)} %copy-done.2, bf16[72,128,128]{2,1,0:T(8,128)(2,1)} %all-to-all-done.1.panel0, ...), custom_call_target="tpu_custom_call" | custom-call | tf_op jit(solution)/shard_map/update/pallas_call | solution.py:206
  (19 shorter events, 0.2 us)
Async XLA Ops:
  6.5 2.2 %copy-start = (bf16[128,128,128]{2,1,0:T(8,128)(2,1)S(1)}, bf16[128,128,128]{2,1,0:T(8,128)(2,1)}, u32[]{:S(2)}) copy-start(bf16[128,128,128]{2,1,0:T(8,128)(2,1)} %tiles.5) | copy-start | bytes 12582916
  8.7 0.7 copy-start.3
  17.5 28.5 %collective-permute-start = (bf16[10,128,128]{2,1,0:T(8,128)(2,1)S(1)}, bf16[10,128,128]{2,1,0:T(8,128)(2,1)}, u32[]{:S(2)}, u32[]{:S(2)}) collective-permute-start(bf16[10,128,128]{2,1,0:T(8,128)(2,1)S(1)} %get-tuple-element.12), channel_id=1, source_target_pairs={{0,192},{16,208},{32,224},{48,240},{1,193},{17,209},{33,225},{49,2... | collective-permute-start | bytes 983048 | tf_op jit(solution)/shard_map/row_scatter/ppermute | solution.py:240
  25.7 20.3 %collective-permute-start.1 = (bf16[10,128,128]{2,1,0:T(8,128)(2,1)S(1)}, bf16[10,128,128]{2,1,0:T(8,128)(2,1)}, u32[]{:S(2)}, u32[]{:S(2)}) collective-permute-start(bf16[10,128,128]{2,1,0:T(8,128)(2,1)S(1)} %get-tuple-element.13), channel_id=1, source_target_pairs={{0,128},{16,144},{32,160},{48,176},{1,129},{17,145},{33,161},{49,1... | collective-permute-start | bytes 983048 | tf_op jit(solution)/shard_map/row_scatter/ppermute | solution.py:240
  28.0 18.0 %collective-permute-start.2 = (bf16[10,128,128]{2,1,0:T(8,128)(2,1)S(1)}, bf16[10,128,128]{2,1,0:T(8,128)(2,1)}, u32[]{:S(2)}, u32[]{:S(2)}) collective-permute-start(bf16[10,128,128]{2,1,0:T(8,128)(2,1)S(1)} %get-tuple-element.14), channel_id=1, source_target_pairs={{0,64},{16,80},{32,96},{48,112},{1,65},{17,81},{33,97},{49,113},{2... | collective-permute-start | bytes 983048 | tf_op jit(solution)/shard_map/row_scatter/ppermute | solution.py:240
  30.0 32.4 %all-to-all-start = ((bf16[64,128,128]{2,1,0:T(8,128)(2,1)}), bf16[64,128,128]{2,1,0:T(8,128)(2,1)S(1)}, u32[]{:S(2)}, u32[]{:S(2)}) async-start(bf16[64,128,128]{2,1,0:T(8,128)(2,1)} %extract_columns.1.after), calls=%async_computation | async-start | bytes 4194304 | tf_op jit(solution)/shard_map/column_scatter/all_to_all | solution.py:243
  36.3 52.4 %all-gather.2.cloned.1.call-start = ((), (), s32[]{:S(2)}) async-start(), calls=%async_computation.2 | async-start | bytes 2359296 | tf_op jit(solution)/shard_map/row_gather/all_gather | solution.py:245
  62.4 5.8 %collective-permute-start.3 = (bf16[2,128,128]{2,1,0:T(8,128)(2,1)S(1)}, bf16[2,128,128]{2,1,0:T(8,128)(2,1)S(1)}, u32[]{:S(2)}, u32[]{:S(2)}) collective-permute-start(bf16[2,128,128]{2,1,0:T(8,128)(2,1)S(1)} %slice.48), channel_id=1, source_target_pairs={{0,32},{16,48},{32,64},{48,80},{64,96},{80,112},{96,128},{112,144}... | collective-permute-start | bytes 196616 | tf_op jit(solution)/shard_map/corner_gather/ppermute | solution.py:250
  68.3 6.4 %collective-permute-start.4 = (bf16[6,128,128]{2,1,0:T(8,128)(2,1)S(1)}, bf16[6,128,128]{2,1,0:T(8,128)(2,1)S(1)}, u32[]{:S(2)}, u32[]{:S(2)}) collective-permute-start(bf16[6,128,128]{2,1,0:T(8,128)(2,1)S(1)} %pad_maximum_fusion.1), channel_id=1, source_target_pairs={{0,4},{1,5},{2,6},{3,7},{4,8},{5,9},{6,10},{7,11},{8,12},{9,13},{1... | collective-permute-start | bytes 589832 | tf_op jit(solution)/shard_map/column_gather/ppermute | solution.py:226
  68.5 19.5 %collective-permute-start.9 = (bf16[4,128,128]{2,1,0:T(8,128)(2,1)S(1)}, bf16[4,128,128]{2,1,0:T(8,128)(2,1)S(1)}, u32[]{:S(2)}, u32[]{:S(2)}) collective-permute-start(bf16[4,128,128]{2,1,0:T(8,128)(2,1)S(1)} %get-tuple-element.21), channel_id=1, source_target_pairs={{0,2},{1,3},{2,0},{3,1},{4,6},{5,7},{6,4},{7,5},{8,10},{9,11},{10,... | collective-permute-start | bytes 393224 | tf_op jit(solution)/shard_map/column_gather/ppermute | solution.py:226
  72.2 15.8 %collective-permute-start.8 = (bf16[4,128,128]{2,1,0:T(8,128)(2,1)S(1)}, bf16[4,128,128]{2,1,0:T(8,128)(2,1)S(1)}, u32[]{:S(2)}, u32[]{:S(2)}) collective-permute-start(bf16[4,128,128]{2,1,0:T(8,128)(2,1)S(1)} %get-tuple-element.21), channel_id=1, source_target_pairs={{0,3},{1,0},{2,1},{3,2},{4,7},{5,4},{6,5},{7,6},{8,11},{9,8},{10,9... | collective-permute-start | bytes 393224 | tf_op jit(solution)/shard_map/column_gather/ppermute | solution.py:226
  72.2 15.8 %collective-permute-start.7 = (bf16[4,128,128]{2,1,0:T(8,128)(2,1)S(1)}, bf16[4,128,128]{2,1,0:T(8,128)(2,1)S(1)}, u32[]{:S(2)}, u32[]{:S(2)}) collective-permute-start(bf16[4,128,128]{2,1,0:T(8,128)(2,1)S(1)} %get-tuple-element.21), channel_id=1, source_target_pairs={{0,1},{1,2},{2,3},{3,0},{4,5},{5,6},{6,7},{7,4},{8,9},{9,10},{10,1... | collective-permute-start | bytes 393224 | tf_op jit(solution)/shard_map/column_gather/ppermute | solution.py:226
  73.7 7.6 %collective-permute-start.6 = (bf16[6,128,128]{2,1,0:T(8,128)(2,1)S(1)}, bf16[6,128,128]{2,1,0:T(8,128)(2,1)S(1)}, u32[]{:S(2)}, u32[]{:S(2)}) collective-permute-start(bf16[6,128,128]{2,1,0:T(8,128)(2,1)S(1)} %pad_maximum_fusion.1), channel_id=1, source_target_pairs={{0,8},{1,9},{2,10},{3,11},{4,12},{5,13},{6,14},{7,15},{8,0},{9,1},... | collective-permute-start | bytes 589832 | tf_op jit(solution)/shard_map/column_gather/ppermute | solution.py:226
  74.6 6.0 %collective-permute-start.5 = (bf16[6,128,128]{2,1,0:T(8,128)(2,1)S(1)}, bf16[6,128,128]{2,1,0:T(8,128)(2,1)S(1)}, u32[]{:S(2)}, u32[]{:S(2)}) collective-permute-start(bf16[6,128,128]{2,1,0:T(8,128)(2,1)S(1)} %pad_maximum_fusion.1), channel_id=1, source_target_pairs={{0,12},{1,13},{2,14},{3,15},{4,0},{5,1},{6,2},{7,3},{8,4},{9,5},{1... | collective-permute-start | bytes 589832 | tf_op jit(solution)/shard_map/column_gather/ppermute | solution.py:226
  83.3 40.8 %copy-start.2 = (bf16[2,256,256]{2,1,0:T(8,128)(2,1)S(1)}, bf16[2,256,256]{2,1,0:T(8,128)(2,1)}, u32[]{:S(2)}) copy-start(bf16[2,256,256]{2,1,0:T(8,128)(2,1)} %inverses.1) | copy-start | bytes 786436
  83.3 40.8 %copy-start.4 = (s32[128,2]{0,1:T(2,128)S(1)}, s32[128,2]{0,1:T(2,128)}, u32[]{:S(2)}) copy-start(s32[128,2]{0,1:T(2,128)} %param.5) | copy-start | bytes 3076
  83.3 40.8 %copy-start.5 = (s32[2,256]{1,0:T(2,128)S(1)}, s32[2,256]{1,0:T(2,128)}, u32[]{:S(2)}) copy-start(s32[2,256]{1,0:T(2,128)} %pivots.1) | copy-start | bytes 6148
  83.3 24.5 %all-to-all-start.1 = ((bf16[72,128,128]{2,1,0:T(8,128)(2,1)}), bf16[72,128,128]{2,1,0:T(8,128)(2,1)}, u32[]{:S(2)}, u32[]{:S(2)}) async-start(bf16[72,128,128]{2,1,0:T(8,128)(2,1)} %bitcast.3), calls=%async_computation.1 | async-start | bytes 4718592 | tf_op jit(solution)/shard_map/column_gather/all_to_all | solution.py:222
  88.7 35.4 %collective-permute-start.13 = (bf16[64,128,128]{2,1,0:T(8,128)(2,1)}, bf16[64,128,128]{2,1,0:T(8,128)(2,1)}, u32[]{:S(2)}, u32[]{:S(2)}) collective-permute-start(bf16[64,128,128]{2,1,0:T(8,128)(2,1)} %all-gather.2.cloned.1.call-done.rows_mine), channel_id=1, source_target_pairs={{0,16},{16,0},{32,48},{48,32},{64,80},{80,64},{96,112},{112,96},{1... | collective-permute-start | bytes 6291464 | tf_op jit(solution)/shard_map/core_swap/ppermute | solution.py:264
  97.5 21.9 %collective-permute-start.12 = (bf16[16,128,128]{2,1,0:T(8,128)(2,1)S(1)}, bf16[16,128,128]{2,1,0:T(8,128)(2,1)S(1)}, u32[]{:S(2)}, u32[]{:S(2)}) collective-permute-start(bf16[16,128,128]{2,1,0:T(8,128)(2,1)S(1)} %pad_maximum_fusion.b0), channel_id=1, source_target_pairs={{0,8},{1,9},{2,10},{3,11},{4,12},{5,13},{6,14},{7,15},{8,0},{9,1},... | collective-permute-start | bytes 1572872 | tf_op jit(solution)/shard_map/column_gather/ppermute | solution.py:226
  97.5 24.8 %collective-permute-start.11 = (bf16[16,128,128]{2,1,0:T(8,128)(2,1)S(1)}, bf16[16,128,128]{2,1,0:T(8,128)(2,1)S(1)}, u32[]{:S(2)}, u32[]{:S(2)}) collective-permute-start(bf16[16,128,128]{2,1,0:T(8,128)(2,1)S(1)} %pad_maximum_fusion.b0), channel_id=1, source_target_pairs={{0,12},{1,13},{2,14},{3,15},{4,0},{5,1},{6,2},{7,3},{8,4},{9,5},{1... | collective-permute-start | bytes 1572872 | tf_op jit(solution)/shard_map/column_gather/ppermute | solution.py:226
  99.2 24.9 %collective-permute-start.10 = (bf16[16,128,128]{2,1,0:T(8,128)(2,1)S(1)}, bf16[16,128,128]{2,1,0:T(8,128)(2,1)S(1)}, u32[]{:S(2)}, u32[]{:S(2)}) collective-permute-start(bf16[16,128,128]{2,1,0:T(8,128)(2,1)S(1)} %pad_maximum_fusion.b0), channel_id=1, source_target_pairs={{0,4},{1,5},{2,6},{3,7},{4,8},{5,9},{6,10},{7,11},{8,12},{9,13},{1... | collective-permute-start | bytes 1572872 | tf_op jit(solution)/shard_map/column_gather/ppermute | solution.py:226
  108.7 15.4 %collective-permute-start.14 = (bf16[4,128,128]{2,1,0:T(8,128)(2,1)S(1)}, bf16[4,128,128]{2,1,0:T(8,128)(2,1)S(1)}, u32[]{:S(2)}, u32[]{:S(2)}) collective-permute-start(bf16[4,128,128]{2,1,0:T(8,128)(2,1)S(1)} %pad_maximum_fusion.2), channel_id=1, source_target_pairs={{0,16},{16,0},{32,48},{48,32},{64,80},{80,64},{96,112},{112,96},{1... | collective-permute-start | bytes 393224 | tf_op jit(solution)/shard_map/core_swap/ppermute | solution.py:265
  124.1 1.6 %copy-start.1 = (bf16[64,128,128]{2,1,0:T(8,128)(2,1)S(1)}, bf16[64,128,128]{2,1,0:T(8,128)(2,1)}, u32[]{:S(2)}) copy-start(bf16[64,128,128]{2,1,0:T(8,128)(2,1)} %all-gather.2.cloned.1.call-done.rows_mine) | copy-start | bytes 6291460
Sparse Core Ops, SparseCore 0:
  46.9 41.6 all-gather.1

commit v2 on v1

--- a/solution.py
+++ b/solution.py
@@ -1,5 +1,3 @@
-import functools
-
 import jax
 import jax.numpy as jnp
 from jax import lax
@@ -13,12 +11,15 @@
 SLOTS = 128
 ROWS = 32
 COLS = 32
+PARTS = 4
 
 
 ALONG_Y = [[x * 4 + y for y in range(4)] for x in range(4)]
 SAME_CORE = [[z * 2 + c for z in range(8)] for c in range(2)]
 SWAP = [(p, p ^ 1) for p in range(16)]
+ALONG_X = [[x * 4 + y for x in range(4)] for y in range(4)]
 UP_Z = [(p, (p + 2) % 16) for p in range(16)]
+UP_Z_SWAP = [(p, (p + 2) % 16 ^ 1) for p in range(16)]
 
 
 def move_x(d):
@@ -35,9 +36,11 @@
 
 VM = pl.BlockSpec(memory_space=pltpu.VMEM)
 SM = pl.BlockSpec(memory_space=pltpu.SMEM)
-
-
-def extract_columns_kernel(pos, tiles, col):
+ANY = pl.BlockSpec(memory_space=pl.ANY)
+HBM = pl.BlockSpec(memory_space=pltpu.HBM)
+
+
+def extract_columns_kernel(pos, tiles, after, col):
     @pl.loop(0, SLOTS)
     def _(s):
         i = pos[0, s]
@@ -48,7 +51,7 @@
             col[(i // 16) * 2 + j % 2] = tiles[s]
 
 
-def extract_rows_kernel(pos, tiles, after, *quarters):
+def extract_rows_kernel(pos, tiles, *quarters):
     @pl.loop(0, SLOTS)
     def _(s):
         i = pos[0, s]
@@ -68,36 +71,41 @@
                     quarters[m][8 + lj] = tiles[s]
 
 
-def extract_columns(pos_t, tiles):
+def extract_columns(pos_t, tiles, after):
     return pl.pallas_call(
         extract_columns_kernel,
         out_shape=jax.ShapeDtypeStruct((2 * ROWS, T, T), BF),
-        in_specs=[SM, VM],
+        in_specs=[SM, VM, ANY],
         out_specs=VM,
         compiler_params=pltpu.CompilerParams(vmem_limit_bytes=16 << 20),
         name="extract_columns",
-    )(pos_t, tiles)
-
-
-def extract_rows(pos_t, tiles, after):
+    )(pos_t, tiles, after)
+
+
+def extract_rows(pos_t, tiles):
     return pl.pallas_call(
         extract_rows_kernel,
         out_shape=[jax.ShapeDtypeStruct((COLS // 4 + 2, T, T), BF)] * 4,
-        in_specs=[SM, VM, pl.BlockSpec(memory_space=pl.ANY)],
+        in_specs=[SM, VM],
         out_specs=[VM] * 4,
         compiler_params=pltpu.CompilerParams(vmem_limit_bytes=16 << 20),
         name="extract_rows",
-    )(pos_t, tiles, after)
+    )(pos_t, tiles)
 
 
 def dot(a, b):
     return jnp.dot(a, b, preferred_element_type=F32)
 
 
-def update_kernel(
-    pos, me, tiles, pivots, inverses, panel0, b0, b1, b2, b3, rows_mine, rows_other, corner_other,
-    out, lc, uc,
-):
+def update_kernel(pos, me, pivots, inverses, *refs):
+    sources, out_hbm = refs[:8], refs[8]
+    held, (out, lc, uc, in_sem, out_sem) = refs[9:17], refs[17:]
+    fetches = [
+        pltpu.make_async_copy(a, b, in_sem.at[n]) for n, (a, b) in enumerate(zip(sources, held))
+    ]
+    for fetch in fetches:
+        fetch.start()
+    panel0, rows_mine, rows_other, *panel1, tiles = held
     p, q = me[0], me[1]
     c = p % 2
     my_x, my_y = q // 4, q % 4
@@ -119,8 +127,26 @@
         low = jnp.concatenate([other[o], other[o + 1]], axis=1)
         return jnp.concatenate([top, low], axis=0)
 
-    low_rows = dot(pair(panel0, 16, corner_other, 0), w0).astype(BF)
-    corner = dot(perm0, pair(panel0, 34, corner_other, 2)).astype(BF)
+    fetches[0].wait()
+    low_rows = dot(pair(panel0, 16, panel0, 18), w0).astype(BF)
+    corner = dot(perm0, pair(panel0, 36, panel0, 38)).astype(BF)
+
+    def blocks(ref, base):
+        rows = [
+            jnp.concatenate([ref[base + 2 * g], ref[base + 2 * g + 1]], axis=1) for g in range(8)
+        ]
+        return jnp.concatenate(rows, axis=0)
+
+    @pl.loop(0, 4)
+    def _(y):
+        low = dot(blocks(panel0, y * 20), w0).astype(BF)
+        for g in range(4):
+            row = 2 * (g * 4 + y)
+            lc[row, :, :256] = low[g * 256 : g * 256 + 128]
+            lc[row + 1, :, :256] = low[g * 256 + 128 : g * 256 + 256]
+
+    fetches[1].wait()
+    fetches[2].wait()
 
     @pl.loop(0, 4)
     def _(m):
@@ -137,23 +163,9 @@
             uc[8 * m + t, :256] = first[:, 128 * t : 128 * t + 128]
             uc[8 * m + t, 256:] = second[:, 128 * t : 128 * t + 128]
 
-    def blocks(ref, base):
-        rows = [
-            jnp.concatenate([ref[base + 2 * g], ref[base + 2 * g + 1]], axis=1) for g in range(8)
-        ]
-        return jnp.concatenate(rows, axis=0)
-
     shifts = (0, 3, 1, 2)
-
-    @pl.loop(0, 4)
-    def _(y):
-        low = dot(blocks(panel0, y * 18), w0).astype(BF)
-        for g, dx in enumerate(shifts):
-            row = 2 * ((my_x + dx) % 4 * 4 + y)
-            lc[row, :, :256] = low[g * 256 : g * 256 + 128]
-            lc[row + 1, :, :256] = low[g * 256 + 128 : g * 256 + 256]
-
-    for ref, dx in zip((b0, b1, b2, b3), shifts):
+    for n, (ref, dx) in enumerate(zip(panel1, shifts)):
+        fetches[3 + n].wait()
         row_of = [2 * ((my_x + dx) % 4 * 4 + (my_y + dy) % 4) for dy in shifts]
         left = jnp.concatenate([lc[r + h, :, :256] for r in row_of for h in range(2)], axis=0)
         new = (blocks(ref, 0).astype(F32) - dot(left, corner)).astype(BF)
@@ -181,40 +193,55 @@
             start = pl.multiple_of((i // 2) * 256 + c * 128, 128)
             out[s] = uc[lj, pl.ds(start, 128), :]
 
-        for t in range(4):
-            @pl.when((i >= 4) & (j == t))
+        @pl.when((i >= 4) & (j < 4))
+        def _():
+            start = pl.multiple_of(j * 128, 128)
+            out[s] = lc[li, :, pl.ds(start, 128)]
+
+    fetches[7].wait()
+    part = SLOTS // PARTS
+    stores = []
+    for n in range(PARTS):
+        @pl.loop(n * part // 8, (n + 1) * part // 8)
+        def _(b):
+            least = jnp.int32(4)
+            for k in range(8):
+                s = b * 8 + k
+                i, j, li, lj = place_of(s)
+                least = jnp.minimum(least, jnp.minimum(i, j))
+                out[s] = (tiles[s].astype(F32) - dot(lc[li], uc[lj])).astype(BF)
+
+            @pl.when(least < 4)
             def _():
-                out[s] = lc[li, :, t * 128 : t * 128 + 128]
-
-    @pl.loop(0, SLOTS // 8)
-    def _(b):
-        least = jnp.int32(4)
-        for k in range(8):
-            s = b * 8 + k
-            i, j, li, lj = place_of(s)
-            least = jnp.minimum(least, jnp.minimum(i, j))
-            out[s] = (tiles[s].astype(F32) - dot(lc[li], uc[lj])).astype(BF)
-
-        @pl.when(least < 4)
-        def _():
-            @pl.loop(b * 8, b * 8 + 8)
-            def _(s):
-                finish(s)
-
-
-def update(*args):
+                @pl.loop(b * 8, b * 8 + 8)
+                def _(s):
+                    finish(s)
+
+        span = pl.ds(n * part, part)
+        store = pltpu.make_async_copy(out.at[span], out_hbm.at[span], out_sem.at[n])
+        store.start()
+        stores.append(store)
+    for store in stores:
+        store.wait()
+
+
+def update(pos_t, me, pivots, inverses, *arrays):
     return pl.pallas_call(
         update_kernel,
         out_shape=jax.ShapeDtypeStruct((SLOTS, T, T), BF),
-        in_specs=[SM, SM] + [VM] * (len(args) - 2),
-        out_specs=VM,
-        scratch_shapes=[
+        in_specs=[SM, SM, VM, VM] + [HBM] * len(arrays),
+        out_specs=HBM,
+        scratch_shapes=[pltpu.VMEM(a.shape, BF) for a in arrays]
+        + [
+            pltpu.VMEM((SLOTS, T, T), BF),
             pltpu.VMEM((ROWS, T, 4 * T), BF),
             pltpu.VMEM((COLS, 4 * T, T), BF),
+            pltpu.SemaphoreType.DMA((len(arrays),)),
+            pltpu.SemaphoreType.DMA((PARTS,)),
         ],
-        compiler_params=pltpu.CompilerParams(vmem_limit_bytes=48 << 20),
+        compiler_params=pltpu.CompilerParams(vmem_limit_bytes=62 << 20),
         name="update",
-    )(*args)
+    )(pos_t, me, pivots, inverses, *arrays)
 
 
 def spread(piece, groups):
@@ -231,8 +258,8 @@
     q = lax.axis_index("pcol")
     pos_t = tile_pos.T
     me = jnp.stack([p, q]).astype(jnp.int32)
-    col = extract_columns(pos_t, tiles)
-    quarters = extract_rows(pos_t, tiles, col)
+    quarters = extract_rows(pos_t, tiles)
+    col = extract_columns(pos_t, tiles, quarters[0])
 
     with jax.named_scope("row_scatter"):
         quarter = quarters[0]
@@ -246,25 +273,26 @@
             quarter[:8], "prow", tiled=True, axis_index_groups=SAME_CORE
         )
     with jax.named_scope("corner_gather"):
-        held, shards = lax.optimization_barrier((quarter[8:], shards))
+        held = quarter[8:]
         below = lax.ppermute(held, "prow", UP_Z)
-        corner = jnp.where((p // 2 + q) % 2 == 1, held, below)
+        below_other = lax.ppermute(held, "prow", UP_Z_SWAP)
+        held_other = lax.ppermute(held, "prow", SWAP)
+        here = (p // 2 + q) % 2 == 1
+        corner = jnp.concatenate(
+            [jnp.where(here, held, below), jnp.where(here, held_other, below_other)]
+        )
     with jax.named_scope("column_gather"):
-        first0 = around(jnp.concatenate([shards[:4], corner]), move_x)
+        first0 = spread(jnp.concatenate([shards[:4], corner]), ALONG_X)
         first1 = jnp.concatenate(around(shards[4:8], move_y))
-        x = q // 4
-        corner = first0[0][4:]
-        for k, g in ((1, 1), (2, 3), (3, 2)):
-            corner = jnp.where(x == k, first0[g][4:], corner)
-        join0 = [g[:4] for g in first0] + [corner]
+        first0, first1 = lax.optimization_barrier((first0, first1))
+        join0 = [first0[8 * x : 8 * x + 4] for x in range(4)] + [first0[4:8]]
         panel0 = spread(jnp.concatenate(join0), ALONG_Y)
         panel1 = around(first1, move_x)
     with jax.named_scope("core_swap"):
-        late, _ = lax.optimization_barrier((rows_mine, first1))
+        late, _, _ = lax.optimization_barrier((rows_mine, panel0, panel1))
         rows_other = lax.ppermute(late, "prow", SWAP)
-        corner_other = lax.ppermute(jnp.concatenate([panel0[16:18], panel0[34:36]]), "prow", SWAP)
     return update(
-        pos_t, me, tiles, pivots, inverses, panel0, *panel1, rows_mine, rows_other, corner_other
+        pos_t, me, pivots, inverses, panel0, rows_mine, rows_other, *panel1, tiles
     )
 
 

time: 159 us -> 156 us (0.981)
  waiting for transfers between devices: 48.8 us -> 62.3 us
  starting transfers between devices: 53.6 us -> 41.3 us
  Pallas kernels: 34.4 us -> 30.2 us
    ppermute x9 -> x6, waiting for transfers between devices: 9.34 us -> 29 us  [around(): return [piece] + [lax.ppermute(piece, 'pcol', move(d)) for d in (1, -1, 2)]]
    all_to_all x1, waiting for transfers between devices: 15.5 us -> 0.01 us  [local(): shards = lax.all_to_all(col, 'pcol', 0, 0, tiled=True)]
    ppermute x1 -> x2, starting transfers between devices: 10.6 us -> 0.78 us  [the longest x1 0.77 us: local(): held_other = lax.ppermute(held, 'prow', SWAP)]
    ppermute x1, starting transfers between devices: 8.82 us -> 2.07 us  [local(): rows_other = lax.ppermute(late, 'prow', SWAP)]
    ppermute x3, waiting for transfers between devices: 9.6 us -> 15.9 us  [local(): got = lax.ppermute(quarters[m], 'prow', scatter_z(m))]
    ppermute x1, waiting for transfers between devices: 5.02 us -> 0.56 us  [local(): below = lax.ppermute(held, 'prow', UP_Z)]
    ppermute x1 -> x2, waiting for transfers between devices: 0.01 us -> 4.34 us  [the longest x1 4.01 us: local(): below_other = lax.ppermute(held, 'prow', UP_Z_SWAP)]
    pallas_call x1, Pallas kernels: 26.3 us -> 22.2 us  [update(): pl.pallas_call(update_kernel, out_shape=jax.ShapeDtypeStruct((SLOTS, T, T...]
  transfers between devices with their start and end apart: 18 -> 17, of which waited for: 9 -> 13; matrix products, arithmetic and copies ran while one was open for 3% -> 2% of each run, Pallas kernels for 0% -> 0%
where the time goes in v2:
time: 156 us; the launch traced here: 155 us
  waiting for transfers between devices  62.3 us (40%)
  starting transfers between devices  41.3 us (26%)
  Pallas kernels  30.2 us (19%)
  between operations  13.5 us (9%)
  local copies, waits for them, and re-layouts  7.06 us (5%)
    ppermute x6, waiting for transfers between devices, around(): return [piece] + [lax.ppermute(piece, 'pcol', move(d)) for d in (1, -1, 2)]  29 us
    pallas_call x1, Pallas kernels, update(): pl.pallas_call(update_kernel, out_shape=jax.ShapeDtypeStruct((SLOTS, T, T...  22.2 us
    ppermute x3, waiting for transfers between devices, local(): got = lax.ppermute(quarters[m], 'prow', scatter_z(m))  15.9 us
    ppermute x3, starting transfers between devices, local(): got = lax.ppermute(quarters[m], 'prow', scatter_z(m))  11.6 us
    all_to_all x2, waiting for transfers between devices, spread(): lax.all_to_all(copies, 'pcol', 0, 0, tiled=True, axis_index_groups=groups)  8.9 us
    all_to_all x2, starting transfers between devices, spread(): lax.all_to_all(copies, 'pcol', 0, 0, tiled=True, axis_index_groups=groups)  8.67 us
    all_to_all x1, starting transfers between devices, local(): shards = lax.all_to_all(col, 'pcol', 0, 0, tiled=True)  7.11 us
    ppermute x6, starting transfers between devices, around(): return [piece] + [lax.ppermute(piece, 'pcol', move(d)) for d in (1, -1, 2)]  7.01 us
  transfers between devices with their start and end apart: 17, of which 13 were waited for; matrix products, arithmetic and copies ran while one was open for 2% of the time, Pallas kernels for 0%

profile of v2, /device:TPU:1, one launch (start us, length us, event | category | flops | bytes accessed | tf_op | source)
XLA Modules:
  0.0 155.3 jit_solution(7418883484365899277)
XLA Ops:
  6.5 2.2 %copy-done = bf16[128,128,128]{2,1,0:T(8,128)(2,1)S(1)} copy-done((bf16[128,128,128]{2,1,0:T(8,128)(2,1)S(1)}, bf16[128,128,128]{2,1,0:T(8,128)(2,1)}, u32[]{:S(2)}) %copy-start) | copy-done | bytes 4194328
  8.7 0.7 copy-done.1
  9.4 3.6 %extract_rows.1 = (bf16[10,128,128]{2,1,0:T(8,128)(2,1)S(1)}, bf16[10,128,128]{2,1,0:T(8,128)(2,1)S(1)}, bf16[10,128,128]{2,1,0:T(8,128)(2,1)S(1)}, bf16[10,128,128]{2,1,0:T(8,128)(2,1)S(1)}) custom-call(s32[2,128]{1,0:T(2,128)S(1)} %bitcast.6, bf16[128,128,128]{2,1,0:T(8,128)(2,1)S(1)} %copy-done), custom_call_target="tpu_custom_call" | custom-call | tf_op jit(solution)/shard_map/extract_rows/pallas_call | solution.py:86
  13.0 4.5 %extract_columns.1 = bf16[64,128,128]{2,1,0:T(8,128)(2,1)} custom-call(s32[2,128]{1,0:T(2,128)S(1)} %bitcast.7, bf16[128,128,128]{2,1,0:T(8,128)(2,1)S(1)} %copy-done, bf16[10,128,128]{2,1,0:T(8,128)(2,1)S(1)} %get-tuple-element.12.after), custom_call_target="tpu_custom_call" | custom-call | tf_op jit(solution)/shard_map/extract_columns/pallas_call | solution.py:75
  17.5 7.1 %all-to-all-start = ((bf16[64,128,128]{2,1,0:T(8,128)(2,1)}), bf16[64,128,128]{2,1,0:T(8,128)(2,1)S(1)}, u32[]{:S(2)}, u32[]{:S(2)}) async-start(bf16[64,128,128]{2,1,0:T(8,128)(2,1)} %extract_columns.1), calls=%async_computation | async-start | bytes 4194304 | tf_op jit(solution)/shard_map/column_scatter/all_to_all | solution.py:270
  24.6 7.4 %collective-permute-start = (bf16[10,128,128]{2,1,0:T(8,128)(2,1)S(1)}, bf16[10,128,128]{2,1,0:T(8,128)(2,1)}, u32[]{:S(2)}, u32[]{:S(2)}) collective-permute-start(bf16[10,128,128]{2,1,0:T(8,128)(2,1)S(1)} %get-tuple-element.13), channel_id=1, source_target_pairs={{0,192},{16,208},{32,224},{48,240},{1,193},{17,209},{33,225},{49,2... | collective-permute-start | bytes 983048 | tf_op jit(solution)/shard_map/row_scatter/ppermute | solution.py:267
  32.0 2.3 %collective-permute-start.1 = (bf16[10,128,128]{2,1,0:T(8,128)(2,1)S(1)}, bf16[10,128,128]{2,1,0:T(8,128)(2,1)}, u32[]{:S(2)}, u32[]{:S(2)}) collective-permute-start(bf16[10,128,128]{2,1,0:T(8,128)(2,1)S(1)} %get-tuple-element.14), channel_id=1, source_target_pairs={{0,128},{16,144},{32,160},{48,176},{1,129},{17,145},{33,161},{49,1... | collective-permute-start | bytes 983048 | tf_op jit(solution)/shard_map/row_scatter/ppermute | solution.py:267
  34.2 2.0 %collective-permute-start.2 = (bf16[10,128,128]{2,1,0:T(8,128)(2,1)S(1)}, bf16[10,128,128]{2,1,0:T(8,128)(2,1)}, u32[]{:S(2)}, u32[]{:S(2)}) collective-permute-start(bf16[10,128,128]{2,1,0:T(8,128)(2,1)S(1)} %get-tuple-element.15), channel_id=1, source_target_pairs={{0,64},{16,80},{32,96},{48,112},{1,65},{17,81},{33,97},{49,113},{2... | collective-permute-start | bytes 983048 | tf_op jit(solution)/shard_map/row_scatter/ppermute | solution.py:267
  36.3 15.9 %collective-permute-done = bf16[10,128,128]{2,1,0:T(8,128)(2,1)} collective-permute-done((bf16[10,128,128]{2,1,0:T(8,128)(2,1)S(1)}, bf16[10,128,128]{2,1,0:T(8,128)(2,1)}, u32[]{:S(2)}, u32[]{:S(2)}) %collective-permute-start) | collective-permute-done | bytes 327712 | tf_op jit(solution)/shard_map/row_scatter/ppermute | solution.py:267
  52.2 0.0 collective-permute-done.1
  52.2 0.0 collective-permute-done.2
  52.2 0.1 select_select_fusion
  52.3 4.0 %collective-permute-start.3 = (bf16[2,128,128]{2,1,0:T(8,128)(2,1)S(1)}, bf16[2,128,128]{2,1,0:T(8,128)(2,1)S(1)}, u32[]{:S(2)}, u32[]{:S(2)}) collective-permute-start(bf16[2,128,128]{2,1,0:T(8,128)(2,1)S(1)} %slice.37), channel_id=1, source_target_pairs={{0,32},{16,48},{32,64},{48,80},{64,96},{80,112},{96,128},{112,144}... | collective-permute-start | bytes 196616 | tf_op jit(solution)/shard_map/corner_gather/ppermute | solution.py:277
  56.3 0.8 collective-permute-start.4
  57.1 0.0 collective-permute-start.5
  57.1 0.6 collective-permute-done.3
  57.7 0.3 collective-permute-done.4
  58.0 4.0 %collective-permute-done.5 = bf16[2,128,128]{2,1,0:T(8,128)(2,1)S(1)} collective-permute-done((bf16[2,128,128]{2,1,0:T(8,128)(2,1)S(1)}, bf16[2,128,128]{2,1,0:T(8,128)(2,1)S(1)}, u32[]{:S(2)}, u32[]{:S(2)}) %collective-permute-start.5) | collective-permute-done | bytes 65568 | tf_op jit(solution)/shard_map/corner_gather/ppermute | solution.py:278
  62.0 0.0 all-to-all-done
  62.1 1.2 broadcast_in_dim.4
  63.3 4.1 %all-to-all-start.1 = ((bf16[32,128,128]{2,1,0:T(8,128)(2,1)}), bf16[32,128,128]{2,1,0:T(8,128)(2,1)S(1)}, u32[]{:S(2)}, u32[]{:S(2)}) async-start(bf16[32,128,128]{2,1,0:T(8,128)(2,1)} %bitcast.3), calls=%async_computation.1 | async-start | bytes 2097152 | tf_op jit(solution)/shard_map/column_gather/all_to_all | solution.py:249
  67.5 0.0 all-gather.2.cloned.1.call-start
  67.5 0.7 slice.39
  68.2 0.0 all-gather.2.cloned.1.call-update
  68.2 2.8 %collective-permute-start.8 = (bf16[4,128,128]{2,1,0:T(8,128)(2,1)S(1)}, bf16[4,128,128]{2,1,0:T(8,128)(2,1)S(1)}, u32[]{:S(2)}, u32[]{:S(2)}) collective-permute-start(bf16[4,128,128]{2,1,0:T(8,128)(2,1)S(1)} %get-tuple-element.19), channel_id=1, source_target_pairs={{0,2},{1,3},{2,0},{3,1},{4,6},{5,7},{6,4},{7,5},{8,10},{9,11},{10,... | collective-permute-start | bytes 393224 | tf_op jit(solution)/shard_map/column_gather/ppermute | solution.py:253
  71.0 0.9 collective-permute-start.7
  71.9 0.6 collective-permute-start.6
  72.4 2.1 %collective-permute-done.8 = bf16[4,128,128]{2,1,0:T(8,128)(2,1)S(1)} collective-permute-done((bf16[4,128,128]{2,1,0:T(8,128)(2,1)S(1)}, bf16[4,128,128]{2,1,0:T(8,128)(2,1)S(1)}, u32[]{:S(2)}, u32[]{:S(2)}) %collective-permute-start.8) | collective-permute-done | bytes 131104 | tf_op jit(solution)/shard_map/column_gather/ppermute | solution.py:253
  74.6 2.8 %collective-permute-done.7 = bf16[4,128,128]{2,1,0:T(8,128)(2,1)S(1)} collective-permute-done((bf16[4,128,128]{2,1,0:T(8,128)(2,1)S(1)}, bf16[4,128,128]{2,1,0:T(8,128)(2,1)S(1)}, u32[]{:S(2)}, u32[]{:S(2)}) %collective-permute-start.7) | collective-permute-done | bytes 131104 | tf_op jit(solution)/shard_map/column_gather/ppermute | solution.py:253
  77.4 0.1 collective-permute-done.6
  77.5 0.1 pad_maximum_fusion.refs_3_
  77.6 0.0 copy-start.2
  77.6 4.8 %all-to-all-done.1 = bf16[32,128,128]{2,1,0:T(8,128)(2,1)S(1)} async-done(((bf16[32,128,128]{2,1,0:T(8,128)(2,1)}), bf16[32,128,128]{2,1,0:T(8,128)(2,1)S(1)}, u32[]{:S(2)}, u32[]{:S(2)}) %all-to-all-start.1) | async-done | bytes 1048608 | tf_op jit(solution)/shard_map/column_gather/all_to_all | solution.py:249
  82.5 2.1 %broadcast_in_dim.5 = bf16[4,20,128,128]{3,2,1,0:T(8,128)(2,1)} broadcast(bf16[20,128,128]{2,1,0:T(8,128)(2,1)S(1)} %slice_dynamic-update-slice_fusion), dimensions={1,2,3} | broadcast | bytes 3276800 | tf_op jit(solution)/shard_map/column_gather/broadcast_in_dim | solution.py:248
  84.6 4.5 %all-to-all-start.2 = ((bf16[80,128,128]{2,1,0:T(8,128)(2,1)}), bf16[80,128,128]{2,1,0:T(8,128)(2,1)}, u32[]{:S(2)}, u32[]{:S(2)}) async-start(bf16[80,128,128]{2,1,0:T(8,128)(2,1)} %bitcast.4), calls=%async_computation.2 | async-start | bytes 5242880 | tf_op jit(solution)/shard_map/column_gather/all_to_all | solution.py:249
  89.2 0.5 collective-permute-start.11
  89.6 2.3 %collective-permute-start.10 = (bf16[16,128,128]{2,1,0:T(8,128)(2,1)S(1)}, bf16[16,128,128]{2,1,0:T(8,128)(2,1)S(1)}, u32[]{:S(2)}, u32[]{:S(2)}) collective-permute-start(bf16[16,128,128]{2,1,0:T(8,128)(2,1)S(1)} %pad_maximum_fusion.refs_3_), channel_id=1, source_target_pairs={{0,12},{1,13},{2,14},{3,15},{4,0},{5,1},{6,2},{7,3},{8,4},{9,5},{1... | collective-permute-start | bytes 1572872 | tf_op jit(solution)/shard_map/column_gather/ppermute | solution.py:253
  91.9 0.0 collective-permute-start.9
  91.9 11.1 %collective-permute-done.11.refs_6_ = bf16[16,128,128]{2,1,0:T(8,128)(2,1)S(1)} collective-permute-done((bf16[16,128,128]{2,1,0:T(8,128)(2,1)S(1)}, bf16[16,128,128]{2,1,0:T(8,128)(2,1)S(1)}, u32[]{:S(2)}, u32[]{:S(2)}) %collective-permute-start.11) | collective-permute-done | bytes 524320 | tf_op jit(solution)/shard_map/column_gather/ppermute | solution.py:253
  103.1 10.2 %collective-permute-done.10.refs_5_ = bf16[16,128,128]{2,1,0:T(8,128)(2,1)S(1)} collective-permute-done((bf16[16,128,128]{2,1,0:T(8,128)(2,1)S(1)}, bf16[16,128,128]{2,1,0:T(8,128)(2,1)S(1)}, u32[]{:S(2)}, u32[]{:S(2)}) %collective-permute-start.10) | collective-permute-done | bytes 524320 | tf_op jit(solution)/shard_map/column_gather/ppermute | solution.py:253
  113.3 2.6 %collective-permute-done.9.refs_4_ = bf16[16,128,128]{2,1,0:T(8,128)(2,1)S(1)} collective-permute-done((bf16[16,128,128]{2,1,0:T(8,128)(2,1)S(1)}, bf16[16,128,128]{2,1,0:T(8,128)(2,1)S(1)}, u32[]{:S(2)}, u32[]{:S(2)}) %collective-permute-start.9) | collective-permute-done | bytes 524320 | tf_op jit(solution)/shard_map/column_gather/ppermute | solution.py:253
  115.9 4.1 %all-to-all-done.2.refs_0_ = bf16[80,128,128]{2,1,0:T(8,128)(2,1)} async-done(((bf16[80,128,128]{2,1,0:T(8,128)(2,1)}), bf16[80,128,128]{2,1,0:T(8,128)(2,1)}, u32[]{:S(2)}, u32[]{:S(2)}) %all-to-all-start.2) | async-done | bytes 2621472 | tf_op jit(solution)/shard_map/column_gather/all_to_all | solution.py:249
  120.1 2.1 %collective-permute-start.12 = (bf16[64,128,128]{2,1,0:T(8,128)(2,1)}, bf16[64,128,128]{2,1,0:T(8,128)(2,1)}, u32[]{:S(2)}, u32[]{:S(2)}) collective-permute-start(bf16[64,128,128]{2,1,0:T(8,128)(2,1)} %all-gather.2.cloned.1.call-done.refs_1_), channel_id=1, source_target_pairs={{0,16},{16,0},{32,48},{48,32},{64,80},{80,64},{96,112},{112,96},{1... | collective-permute-start | bytes 6291464 | tf_op jit(solution)/shard_map/core_swap/ppermute | solution.py:293
  122.1 0.6 pad_add_fusion.me
  122.8 3.5 %collective-permute-done.12.refs_2_ = bf16[64,128,128]{2,1,0:T(8,128)(2,1)} collective-permute-done((bf16[64,128,128]{2,1,0:T(8,128)(2,1)}, bf16[64,128,128]{2,1,0:T(8,128)(2,1)}, u32[]{:S(2)}, u32[]{:S(2)}) %collective-permute-start.12) | collective-permute-done | bytes 2097184 | tf_op jit(solution)/shard_map/core_swap/ppermute | solution.py:293
  126.3 0.0 copy-done.3
  126.3 0.0 copy-done.5
  126.3 22.2 %update.1 = bf16[128,128,128]{2,1,0:T(8,128)(2,1)} custom-call(s32[2,128]{1,0:T(2,128)} %bitcast.5, s32[2]{0:T(128)} %pad_add_fusion.me, s32[2,256]{1,0:T(2,128)} %pivots.1, bf16[2,256,256]{2,1,0:T(8,128)(2,1)} %inverses.1, bf16[80,128,128]{2,1,0:T(8,128)(2,1)} %all-to-all-done.2.refs_0_, bf16[64,128,128]{2,1,0:T(8,128)(2,1)} %all-gather.2.cloned.1.call-done.refs_1_, ...), custom_call_target="tpu_custom_call" | custom-call | tf_op jit(solution)/shard_map/update/pallas_call | solution.py:229
  (18 shorter events, 0.2 us)
Async XLA Ops:
  6.5 2.2 %copy-start = (bf16[128,128,128]{2,1,0:T(8,128)(2,1)S(1)}, bf16[128,128,128]{2,1,0:T(8,128)(2,1)}, u32[]{:S(2)}) copy-start(bf16[128,128,128]{2,1,0:T(8,128)(2,1)} %refs_7_.1) | copy-start | bytes 12582916
  8.7 0.7 copy-start.1
  17.5 44.5 %all-to-all-start = ((bf16[64,128,128]{2,1,0:T(8,128)(2,1)}), bf16[64,128,128]{2,1,0:T(8,128)(2,1)S(1)}, u32[]{:S(2)}, u32[]{:S(2)}) async-start(bf16[64,128,128]{2,1,0:T(8,128)(2,1)} %extract_columns.1), calls=%async_computation | async-start | bytes 4194304 | tf_op jit(solution)/shard_map/column_scatter/all_to_all | solution.py:270
  24.6 27.6 %collective-permute-start = (bf16[10,128,128]{2,1,0:T(8,128)(2,1)S(1)}, bf16[10,128,128]{2,1,0:T(8,128)(2,1)}, u32[]{:S(2)}, u32[]{:S(2)}) collective-permute-start(bf16[10,128,128]{2,1,0:T(8,128)(2,1)S(1)} %get-tuple-element.13), channel_id=1, source_target_pairs={{0,192},{16,208},{32,224},{48,240},{1,193},{17,209},{33,225},{49,2... | collective-permute-start | bytes 983048 | tf_op jit(solution)/shard_map/row_scatter/ppermute | solution.py:267
  32.0 20.2 %collective-permute-start.1 = (bf16[10,128,128]{2,1,0:T(8,128)(2,1)S(1)}, bf16[10,128,128]{2,1,0:T(8,128)(2,1)}, u32[]{:S(2)}, u32[]{:S(2)}) collective-permute-start(bf16[10,128,128]{2,1,0:T(8,128)(2,1)S(1)} %get-tuple-element.14), channel_id=1, source_target_pairs={{0,128},{16,144},{32,160},{48,176},{1,129},{17,145},{33,161},{49,1... | collective-permute-start | bytes 983048 | tf_op jit(solution)/shard_map/row_scatter/ppermute | solution.py:267
  34.2 18.0 %collective-permute-start.2 = (bf16[10,128,128]{2,1,0:T(8,128)(2,1)S(1)}, bf16[10,128,128]{2,1,0:T(8,128)(2,1)}, u32[]{:S(2)}, u32[]{:S(2)}) collective-permute-start(bf16[10,128,128]{2,1,0:T(8,128)(2,1)S(1)} %get-tuple-element.15), channel_id=1, source_target_pairs={{0,64},{16,80},{32,96},{48,112},{1,65},{17,81},{33,97},{49,113},{2... | collective-permute-start | bytes 983048 | tf_op jit(solution)/shard_map/row_scatter/ppermute | solution.py:267
  52.3 5.3 %collective-permute-start.3 = (bf16[2,128,128]{2,1,0:T(8,128)(2,1)S(1)}, bf16[2,128,128]{2,1,0:T(8,128)(2,1)S(1)}, u32[]{:S(2)}, u32[]{:S(2)}) collective-permute-start(bf16[2,128,128]{2,1,0:T(8,128)(2,1)S(1)} %slice.37), channel_id=1, source_target_pairs={{0,32},{16,48},{32,64},{48,80},{64,96},{80,112},{96,128},{112,144}... | collective-permute-start | bytes 196616 | tf_op jit(solution)/shard_map/corner_gather/ppermute | solution.py:277
  56.3 1.7 %collective-permute-start.4 = (bf16[2,128,128]{2,1,0:T(8,128)(2,1)S(1)}, bf16[2,128,128]{2,1,0:T(8,128)(2,1)S(1)}, u32[]{:S(2)}, u32[]{:S(2)}) collective-permute-start(bf16[2,128,128]{2,1,0:T(8,128)(2,1)S(1)} %slice.37), channel_id=1, source_target_pairs={{0,16},{16,0},{32,48},{48,32},{64,80},{80,64},{96,112},{112,96},{1... | collective-permute-start | bytes 196616 | tf_op jit(solution)/shard_map/corner_gather/ppermute | solution.py:279
  57.1 4.9 %collective-permute-start.5 = (bf16[2,128,128]{2,1,0:T(8,128)(2,1)S(1)}, bf16[2,128,128]{2,1,0:T(8,128)(2,1)S(1)}, u32[]{:S(2)}, u32[]{:S(2)}) collective-permute-start(bf16[2,128,128]{2,1,0:T(8,128)(2,1)S(1)} %slice.37), channel_id=1, source_target_pairs={{0,48},{16,32},{32,80},{48,64},{64,112},{80,96},{96,144},{112,128}... | collective-permute-start | bytes 196616 | tf_op jit(solution)/shard_map/corner_gather/ppermute | solution.py:278
  63.3 19.0 %all-to-all-start.1 = ((bf16[32,128,128]{2,1,0:T(8,128)(2,1)}), bf16[32,128,128]{2,1,0:T(8,128)(2,1)S(1)}, u32[]{:S(2)}, u32[]{:S(2)}) async-start(bf16[32,128,128]{2,1,0:T(8,128)(2,1)} %bitcast.3), calls=%async_computation.1 | async-start | bytes 2097152 | tf_op jit(solution)/shard_map/column_gather/all_to_all | solution.py:249
  67.5 48.5 %all-gather.2.cloned.1.call-start = ((), (), s32[]{:S(2)}) async-start(), calls=%async_computation.3 | async-start | bytes 2359296 | tf_op jit(solution)/shard_map/row_gather/all_gather | solution.py:272
  68.2 6.4 %collective-permute-start.8 = (bf16[4,128,128]{2,1,0:T(8,128)(2,1)S(1)}, bf16[4,128,128]{2,1,0:T(8,128)(2,1)S(1)}, u32[]{:S(2)}, u32[]{:S(2)}) collective-permute-start(bf16[4,128,128]{2,1,0:T(8,128)(2,1)S(1)} %get-tuple-element.19), channel_id=1, source_target_pairs={{0,2},{1,3},{2,0},{3,1},{4,6},{5,7},{6,4},{7,5},{8,10},{9,11},{10,... | collective-permute-start | bytes 393224 | tf_op jit(solution)/shard_map/column_gather/ppermute | solution.py:253
  71.0 6.4 %collective-permute-start.7 = (bf16[4,128,128]{2,1,0:T(8,128)(2,1)S(1)}, bf16[4,128,128]{2,1,0:T(8,128)(2,1)S(1)}, u32[]{:S(2)}, u32[]{:S(2)}) collective-permute-start(bf16[4,128,128]{2,1,0:T(8,128)(2,1)S(1)} %get-tuple-element.19), channel_id=1, source_target_pairs={{0,3},{1,0},{2,1},{3,2},{4,7},{5,4},{6,5},{7,6},{8,11},{9,8},{10,9... | collective-permute-start | bytes 393224 | tf_op jit(solution)/shard_map/column_gather/ppermute | solution.py:253
  71.9 5.6 %collective-permute-start.6 = (bf16[4,128,128]{2,1,0:T(8,128)(2,1)S(1)}, bf16[4,128,128]{2,1,0:T(8,128)(2,1)S(1)}, u32[]{:S(2)}, u32[]{:S(2)}) collective-permute-start(bf16[4,128,128]{2,1,0:T(8,128)(2,1)S(1)} %get-tuple-element.19), channel_id=1, source_target_pairs={{0,1},{1,2},{2,3},{3,0},{4,5},{5,6},{6,7},{7,4},{8,9},{9,10},{10,1... | collective-permute-start | bytes 393224 | tf_op jit(solution)/shard_map/column_gather/ppermute | solution.py:253
  77.6 14.4 %copy-start.2 = (bf16[16,128,128]{2,1,0:T(8,128)(2,1)}, bf16[16,128,128]{2,1,0:T(8,128)(2,1)S(1)}, u32[]{:S(2)}) copy-start(bf16[16,128,128]{2,1,0:T(8,128)(2,1)S(1)} %pad_maximum_fusion.refs_3_) | copy-start | bytes 1572868
  84.6 35.4 %all-to-all-start.2 = ((bf16[80,128,128]{2,1,0:T(8,128)(2,1)}), bf16[80,128,128]{2,1,0:T(8,128)(2,1)}, u32[]{:S(2)}, u32[]{:S(2)}) async-start(bf16[80,128,128]{2,1,0:T(8,128)(2,1)} %bitcast.4), calls=%async_computation.2 | async-start | bytes 5242880 | tf_op jit(solution)/shard_map/column_gather/all_to_all | solution.py:249
  89.2 13.9 %collective-permute-start.11 = (bf16[16,128,128]{2,1,0:T(8,128)(2,1)S(1)}, bf16[16,128,128]{2,1,0:T(8,128)(2,1)S(1)}, u32[]{:S(2)}, u32[]{:S(2)}) collective-permute-start(bf16[16,128,128]{2,1,0:T(8,128)(2,1)S(1)} %pad_maximum_fusion.refs_3_), channel_id=1, source_target_pairs={{0,8},{1,9},{2,10},{3,11},{4,12},{5,13},{6,14},{7,15},{8,0},{9,1},... | collective-permute-start | bytes 1572872 | tf_op jit(solution)/shard_map/column_gather/ppermute | solution.py:253
  89.6 23.7 %collective-permute-start.10 = (bf16[16,128,128]{2,1,0:T(8,128)(2,1)S(1)}, bf16[16,128,128]{2,1,0:T(8,128)(2,1)S(1)}, u32[]{:S(2)}, u32[]{:S(2)}) collective-permute-start(bf16[16,128,128]{2,1,0:T(8,128)(2,1)S(1)} %pad_maximum_fusion.refs_3_), channel_id=1, source_target_pairs={{0,12},{1,13},{2,14},{3,15},{4,0},{5,1},{6,2},{7,3},{8,4},{9,5},{1... | collective-permute-start | bytes 1572872 | tf_op jit(solution)/shard_map/column_gather/ppermute | solution.py:253
  91.9 24.0 %collective-permute-start.9 = (bf16[16,128,128]{2,1,0:T(8,128)(2,1)S(1)}, bf16[16,128,128]{2,1,0:T(8,128)(2,1)S(1)}, u32[]{:S(2)}, u32[]{:S(2)}) collective-permute-start(bf16[16,128,128]{2,1,0:T(8,128)(2,1)S(1)} %pad_maximum_fusion.refs_3_), channel_id=1, source_target_pairs={{0,4},{1,5},{2,6},{3,7},{4,8},{5,9},{6,10},{7,11},{8,12},{9,13},{1... | collective-permute-start | bytes 1572872 | tf_op jit(solution)/shard_map/column_gather/ppermute | solution.py:253
  103.1 23.2 %copy-start.3 = (bf16[16,128,128]{2,1,0:T(8,128)(2,1)}, bf16[16,128,128]{2,1,0:T(8,128)(2,1)S(1)}, u32[]{:S(2)}) copy-start(bf16[16,128,128]{2,1,0:T(8,128)(2,1)S(1)} %collective-permute-done.11.refs_6_) | copy-start | bytes 1572868
  113.3 12.9 %copy-start.4 = (bf16[16,128,128]{2,1,0:T(8,128)(2,1)}, bf16[16,128,128]{2,1,0:T(8,128)(2,1)S(1)}, u32[]{:S(2)}) copy-start(bf16[16,128,128]{2,1,0:T(8,128)(2,1)S(1)} %collective-permute-done.10.refs_5_) | copy-start | bytes 1572868
  115.9 10.3 %copy-start.5 = (bf16[16,128,128]{2,1,0:T(8,128)(2,1)}, bf16[16,128,128]{2,1,0:T(8,128)(2,1)S(1)}, u32[]{:S(2)}) copy-start(bf16[16,128,128]{2,1,0:T(8,128)(2,1)S(1)} %collective-permute-done.9.refs_4_) | copy-start | bytes 1572868
  120.1 6.2 %collective-permute-start.12 = (bf16[64,128,128]{2,1,0:T(8,128)(2,1)}, bf16[64,128,128]{2,1,0:T(8,128)(2,1)}, u32[]{:S(2)}, u32[]{:S(2)}) collective-permute-start(bf16[64,128,128]{2,1,0:T(8,128)(2,1)} %all-gather.2.cloned.1.call-done.refs_1_), channel_id=1, source_target_pairs={{0,16},{16,0},{32,48},{48,32},{64,80},{80,64},{96,112},{112,96},{1... | collective-permute-start | bytes 6291464 | tf_op jit(solution)/shard_map/core_swap/ppermute | solution.py:293
Sparse Core Ops, SparseCore 0:
  70.1 37.7 all-gather.1

commit v3 on v2

--- a/solution.py
+++ b/solution.py
@@ -19,7 +19,6 @@
 SWAP = [(p, p ^ 1) for p in range(16)]
 ALONG_X = [[x * 4 + y for x in range(4)] for y in range(4)]
 UP_Z = [(p, (p + 2) % 16) for p in range(16)]
-UP_Z_SWAP = [(p, (p + 2) % 16 ^ 1) for p in range(16)]
 
 
 def move_x(d):
@@ -98,14 +97,14 @@
 
 
 def update_kernel(pos, me, pivots, inverses, *refs):
-    sources, out_hbm = refs[:8], refs[8]
-    held, (out, lc, uc, in_sem, out_sem) = refs[9:17], refs[17:]
+    sources, out_hbm = refs[:9], refs[9]
+    held, (out, lc, uc, in_sem, out_sem) = refs[10:19], refs[19:]
     fetches = [
         pltpu.make_async_copy(a, b, in_sem.at[n]) for n, (a, b) in enumerate(zip(sources, held))
     ]
     for fetch in fetches:
         fetch.start()
-    panel0, rows_mine, rows_other, *panel1, tiles = held
+    panel0, rows_mine, rows_other, *panel1, tiles, corner_other = held
     p, q = me[0], me[1]
     c = p % 2
     my_x, my_y = q // 4, q % 4
@@ -128,8 +127,9 @@
         return jnp.concatenate([top, low], axis=0)
 
     fetches[0].wait()
-    low_rows = dot(pair(panel0, 16, panel0, 18), w0).astype(BF)
-    corner = dot(perm0, pair(panel0, 36, panel0, 38)).astype(BF)
+    fetches[8].wait()
+    low_rows = dot(pair(panel0, 16, corner_other, 0), w0).astype(BF)
+    corner = dot(perm0, pair(panel0, 34, corner_other, 2)).astype(BF)
 
     def blocks(ref, base):
         rows = [
@@ -139,7 +139,7 @@
 
     @pl.loop(0, 4)
     def _(y):
-        low = dot(blocks(panel0, y * 20), w0).astype(BF)
+        low = dot(blocks(panel0, y * 18), w0).astype(BF)
         for g in range(4):
             row = 2 * (g * 4 + y)
             lc[row, :, :256] = low[g * 256 : g * 256 + 128]
@@ -275,24 +275,22 @@
     with jax.named_scope("corner_gather"):
         held = quarter[8:]
         below = lax.ppermute(held, "prow", UP_Z)
-        below_other = lax.ppermute(held, "prow", UP_Z_SWAP)
-        held_other = lax.ppermute(held, "prow", SWAP)
-        here = (p // 2 + q) % 2 == 1
-        corner = jnp.concatenate(
-            [jnp.where(here, held, below), jnp.where(here, held_other, below_other)]
-        )
+        corner = jnp.where((p // 2 + q) % 2 == 1, held, below)
     with jax.named_scope("column_gather"):
         first0 = spread(jnp.concatenate([shards[:4], corner]), ALONG_X)
         first1 = jnp.concatenate(around(shards[4:8], move_y))
         first0, first1 = lax.optimization_barrier((first0, first1))
-        join0 = [first0[8 * x : 8 * x + 4] for x in range(4)] + [first0[4:8]]
+        join0 = [first0[6 * x : 6 * x + 4] for x in range(4)] + [first0[4:6]]
         panel0 = spread(jnp.concatenate(join0), ALONG_Y)
         panel1 = around(first1, move_x)
     with jax.named_scope("core_swap"):
-        late, _, _ = lax.optimization_barrier((rows_mine, panel0, panel1))
+        late, _ = lax.optimization_barrier((rows_mine, panel1))
         rows_other = lax.ppermute(late, "prow", SWAP)
+        corner_other = lax.ppermute(
+            jnp.concatenate([panel0[16:18], panel0[34:36]]), "prow", SWAP
+        )
     return update(
-        pos_t, me, pivots, inverses, panel0, rows_mine, rows_other, *panel1, tiles
+        pos_t, me, pivots, inverses, panel0, rows_mine, rows_other, *panel1, tiles, corner_other
     )
 
 

time: 156 us -> 151 us (0.968)
  waiting for transfers between devices: 62.3 us -> 44.8 us
  starting transfers between devices: 41.3 us -> 49.6 us
  Pallas kernels: 30.2 us -> 33.1 us
  local copies, waits for them, and re-layouts: 7.06 us -> 8.83 us
    all_to_all x1, waiting for transfers between devices: 0.01 us -> 14.7 us  [local(): shards = lax.all_to_all(col, 'pcol', 0, 0, tiled=True)]
    ppermute x3, waiting for transfers between devices: 15.9 us -> 5.13 us  [local(): got = lax.ppermute(quarters[m], 'prow', scatter_z(m))]
    ppermute x6, waiting for transfers between devices: 29 us -> 20.2 us  [around(): return [piece] + [lax.ppermute(piece, 'pcol', move(d)) for d in (1, -1, 2)]]
    ppermute x2 -> x1, starting transfers between devices: 0.78 us -> 8.83 us  [local(): lax.ppermute(jnp.concatenate([panel0[16:18], panel0[34:36]]), 'prow', SWAP)]
    all_to_all x2, waiting for transfers between devices: 8.9 us -> 3.03 us  [spread(): lax.all_to_all(copies, 'pcol', 0, 0, tiled=True, axis_index_groups=groups)]
    ppermute x2 -> x1, waiting for transfers between devices: 4.34 us -> 0.32 us  [local(): lax.ppermute(jnp.concatenate([panel0[16:18], panel0[34:36]]), 'prow', SWAP)]
    ppermute x1, waiting for transfers between devices: 3.49 us -> 0.01 us  [local(): rows_other = lax.ppermute(late, 'prow', SWAP)]
    pallas_call x1, Pallas kernels: 22.2 us -> 25.1 us  [update(): pl.pallas_call(update_kernel, out_shape=jax.ShapeDtypeStruct((SLOTS, T, T...]
  transfers between devices with their start and end apart: 17 -> 16, of which waited for: 13 -> 12; matrix products, arithmetic and copies ran while one was open for 2% -> 3% of each run, Pallas kernels for 0% -> 3%
where the time goes in v3:
time: 151 us
  starting transfers between devices  49.6 us (33%)
  waiting for transfers between devices  44.8 us (30%)
  Pallas kernels  33.1 us (22%)
  between operations  13.6 us (9%)
  local copies, waits for them, and re-layouts  8.83 us (6%)
    pallas_call x1, Pallas kernels, update(): pl.pallas_call(update_kernel, out_shape=jax.ShapeDtypeStruct((SLOTS, T, T...  25.1 us
    ppermute x6, waiting for transfers between devices, around(): return [piece] + [lax.ppermute(piece, 'pcol', move(d)) for d in (1, -1, 2)]  20.2 us
    all_to_all x1, waiting for transfers between devices, local(): shards = lax.all_to_all(col, 'pcol', 0, 0, tiled=True)  14.7 us
    ppermute x3, starting transfers between devices, local(): got = lax.ppermute(quarters[m], 'prow', scatter_z(m))  12.5 us
    ppermute x1, starting transfers between devices, local(): lax.ppermute(jnp.concatenate([panel0[16:18], panel0[34:36]]), 'prow', SWAP)  8.83 us
    ppermute x6, starting transfers between devices, around(): return [piece] + [lax.ppermute(piece, 'pcol', move(d)) for d in (1, -1, 2)]  8.01 us
    all_to_all x2, starting transfers between devices, spread(): lax.all_to_all(copies, 'pcol', 0, 0, tiled=True, axis_index_groups=groups)  7.13 us
    all_to_all x1, starting transfers between devices, local(): shards = lax.all_to_all(col, 'pcol', 0, 0, tiled=True)  6.28 us
  transfers between devices with their start and end apart: 16, of which 12 were waited for; matrix products, arithmetic and copies ran while one was open for 3% of the time, Pallas kernels for 3%

profile of v3, /device:TPU:1, one launch (start us, length us, event | category | flops | bytes accessed | tf_op | source)
XLA Modules:
  0.0 150.8 jit_solution(7051798917996360134)
XLA Ops:
  6.5 2.2 %copy-done = bf16[128,128,128]{2,1,0:T(8,128)(2,1)S(1)} copy-done((bf16[128,128,128]{2,1,0:T(8,128)(2,1)S(1)}, bf16[128,128,128]{2,1,0:T(8,128)(2,1)}, u32[]{:S(2)}) %copy-start) | copy-done | bytes 4194328
  8.7 0.7 copy-done.1
  9.4 3.6 %extract_rows.1 = (bf16[10,128,128]{2,1,0:T(8,128)(2,1)S(1)}, bf16[10,128,128]{2,1,0:T(8,128)(2,1)S(1)}, bf16[10,128,128]{2,1,0:T(8,128)(2,1)S(1)}, bf16[10,128,128]{2,1,0:T(8,128)(2,1)S(1)}) custom-call(s32[2,128]{1,0:T(2,128)S(1)} %bitcast.6, bf16[128,128,128]{2,1,0:T(8,128)(2,1)S(1)} %copy-done), custom_call_target="tpu_custom_call" | custom-call | tf_op jit(solution)/shard_map/extract_rows/pallas_call | solution.py:85
  13.0 8.2 %collective-permute-start = (bf16[10,128,128]{2,1,0:T(8,128)(2,1)S(1)}, bf16[10,128,128]{2,1,0:T(8,128)(2,1)}, u32[]{:S(2)}, u32[]{:S(2)}) collective-permute-start(bf16[10,128,128]{2,1,0:T(8,128)(2,1)S(1)} %get-tuple-element.13), channel_id=1, source_target_pairs={{0,192},{16,208},{32,224},{48,240},{1,193},{17,209},{33,225},{49,2... | collective-permute-start | bytes 983048 | tf_op jit(solution)/shard_map/row_scatter/ppermute | solution.py:267
  21.2 2.3 %collective-permute-start.1 = (bf16[10,128,128]{2,1,0:T(8,128)(2,1)S(1)}, bf16[10,128,128]{2,1,0:T(8,128)(2,1)}, u32[]{:S(2)}, u32[]{:S(2)}) collective-permute-start(bf16[10,128,128]{2,1,0:T(8,128)(2,1)S(1)} %get-tuple-element.14), channel_id=1, source_target_pairs={{0,128},{16,144},{32,160},{48,176},{1,129},{17,145},{33,161},{49,1... | collective-permute-start | bytes 983048 | tf_op jit(solution)/shard_map/row_scatter/ppermute | solution.py:267
  23.5 2.0 %collective-permute-start.2 = (bf16[10,128,128]{2,1,0:T(8,128)(2,1)S(1)}, bf16[10,128,128]{2,1,0:T(8,128)(2,1)}, u32[]{:S(2)}, u32[]{:S(2)}) collective-permute-start(bf16[10,128,128]{2,1,0:T(8,128)(2,1)S(1)} %get-tuple-element.15), channel_id=1, source_target_pairs={{0,64},{16,80},{32,96},{48,112},{1,65},{17,81},{33,97},{49,113},{2... | collective-permute-start | bytes 983048 | tf_op jit(solution)/shard_map/row_scatter/ppermute | solution.py:267
  25.5 4.5 %extract_columns.1 = bf16[64,128,128]{2,1,0:T(8,128)(2,1)} custom-call(s32[2,128]{1,0:T(2,128)S(1)} %bitcast.7, bf16[128,128,128]{2,1,0:T(8,128)(2,1)S(1)} %copy-done, bf16[10,128,128]{2,1,0:T(8,128)(2,1)S(1)} %get-tuple-element.12.after), custom_call_target="tpu_custom_call" | custom-call | tf_op jit(solution)/shard_map/extract_columns/pallas_call | solution.py:74
  30.0 6.3 %all-to-all-start = ((bf16[64,128,128]{2,1,0:T(8,128)(2,1)}), bf16[64,128,128]{2,1,0:T(8,128)(2,1)S(1)}, u32[]{:S(2)}, u32[]{:S(2)}) async-start(bf16[64,128,128]{2,1,0:T(8,128)(2,1)} %extract_columns.1), calls=%async_computation | async-start | bytes 4194304 | tf_op jit(solution)/shard_map/column_scatter/all_to_all | solution.py:270
  36.3 0.0 all-gather.2.cloned.1.call-start
  36.3 5.1 %collective-permute-done = bf16[10,128,128]{2,1,0:T(8,128)(2,1)} collective-permute-done((bf16[10,128,128]{2,1,0:T(8,128)(2,1)S(1)}, bf16[10,128,128]{2,1,0:T(8,128)(2,1)}, u32[]{:S(2)}, u32[]{:S(2)}) %collective-permute-start) | collective-permute-done | bytes 327712 | tf_op jit(solution)/shard_map/row_scatter/ppermute | solution.py:267
  41.5 0.0 collective-permute-done.1
  41.5 0.0 collective-permute-done.2
  41.5 0.1 select_select_fusion
  41.5 0.7 slice.47
  42.3 0.0 all-gather.2.cloned.1.call-update
  42.3 4.0 %collective-permute-start.3 = (bf16[2,128,128]{2,1,0:T(8,128)(2,1)S(1)}, bf16[2,128,128]{2,1,0:T(8,128)(2,1)S(1)}, u32[]{:S(2)}, u32[]{:S(2)}) collective-permute-start(bf16[2,128,128]{2,1,0:T(8,128)(2,1)S(1)} %slice.45), channel_id=1, source_target_pairs={{0,32},{16,48},{32,64},{48,80},{64,96},{80,112},{96,128},{112,144}... | collective-permute-start | bytes 196616 | tf_op jit(solution)/shard_map/corner_gather/ppermute | solution.py:277
  46.3 1.3 collective-permute-done.3
  47.6 14.7 %all-to-all-done = bf16[64,128,128]{2,1,0:T(8,128)(2,1)S(1)} async-done(((bf16[64,128,128]{2,1,0:T(8,128)(2,1)}), bf16[64,128,128]{2,1,0:T(8,128)(2,1)S(1)}, u32[]{:S(2)}, u32[]{:S(2)}) %all-to-all-start) | async-done | bytes 2097184 | tf_op jit(solution)/shard_map/column_scatter/all_to_all | solution.py:270
  62.4 1.0 broadcast_in_dim.4
  63.5 3.5 %all-to-all-start.1 = ((bf16[24,128,128]{2,1,0:T(8,128)(2,1)}), bf16[24,128,128]{2,1,0:T(8,128)(2,1)S(1)}, u32[]{:S(2)}, u32[]{:S(2)}) async-start(bf16[24,128,128]{2,1,0:T(8,128)(2,1)} %bitcast.3), calls=%async_computation.1 | async-start | bytes 1572864 | tf_op jit(solution)/shard_map/column_gather/all_to_all | solution.py:249
  67.0 2.2 %collective-permute-start.6 = (bf16[4,128,128]{2,1,0:T(8,128)(2,1)S(1)}, bf16[4,128,128]{2,1,0:T(8,128)(2,1)S(1)}, u32[]{:S(2)}, u32[]{:S(2)}) collective-permute-start(bf16[4,128,128]{2,1,0:T(8,128)(2,1)S(1)} %get-tuple-element.21), channel_id=1, source_target_pairs={{0,2},{1,3},{2,0},{3,1},{4,6},{5,7},{6,4},{7,5},{8,10},{9,11},{10,... | collective-permute-start | bytes 393224 | tf_op jit(solution)/shard_map/column_gather/ppermute | solution.py:253
  69.2 0.6 collective-permute-start.5
  69.8 0.9 collective-permute-start.4
  70.7 1.7 %collective-permute-done.6 = bf16[4,128,128]{2,1,0:T(8,128)(2,1)S(1)} collective-permute-done((bf16[4,128,128]{2,1,0:T(8,128)(2,1)S(1)}, bf16[4,128,128]{2,1,0:T(8,128)(2,1)S(1)}, u32[]{:S(2)}, u32[]{:S(2)}) %collective-permute-start.6) | collective-permute-done | bytes 131104 | tf_op jit(solution)/shard_map/column_gather/ppermute | solution.py:253
  72.4 1.0 collective-permute-done.5
  73.4 1.8 %collective-permute-done.4 = bf16[4,128,128]{2,1,0:T(8,128)(2,1)S(1)} collective-permute-done((bf16[4,128,128]{2,1,0:T(8,128)(2,1)S(1)}, bf16[4,128,128]{2,1,0:T(8,128)(2,1)S(1)}, u32[]{:S(2)}, u32[]{:S(2)}) %collective-permute-start.4) | collective-permute-done | bytes 131104 | tf_op jit(solution)/shard_map/column_gather/ppermute | solution.py:253
  75.2 0.1 pad_maximum_fusion.refs_3_
  75.3 0.0 copy-start.3
  75.3 0.1 all-to-all-done.1
  75.3 2.9 %collective-permute-start.9 = (bf16[16,128,128]{2,1,0:T(8,128)(2,1)S(1)}, bf16[16,128,128]{2,1,0:T(8,128)(2,1)S(1)}, u32[]{:S(2)}, u32[]{:S(2)}) collective-permute-start(bf16[16,128,128]{2,1,0:T(8,128)(2,1)S(1)} %pad_maximum_fusion.refs_3_), channel_id=1, source_target_pairs={{0,8},{1,9},{2,10},{3,11},{4,12},{5,13},{6,14},{7,15},{8,0},{9,1},... | collective-permute-start | bytes 1572872 | tf_op jit(solution)/shard_map/column_gather/ppermute | solution.py:253
  78.2 0.9 collective-permute-start.8
  79.1 0.6 collective-permute-start.7
  79.8 2.0 %broadcast_in_dim.5 = bf16[4,18,128,128]{3,2,1,0:T(8,128)(2,1)} broadcast(bf16[18,128,128]{2,1,0:T(8,128)(2,1)S(1)} %slice_dynamic-update-slice_fusion.4), dimensions={1,2,3} | broadcast | bytes 2949120 | tf_op jit(solution)/shard_map/column_gather/broadcast_in_dim | solution.py:248
  81.8 0.0 copy-done.3
  81.8 3.6 %all-to-all-start.2 = ((bf16[72,128,128]{2,1,0:T(8,128)(2,1)}), bf16[72,128,128]{2,1,0:T(8,128)(2,1)S(1)}, u32[]{:S(2)}, u32[]{:S(2)}) async-start(bf16[72,128,128]{2,1,0:T(8,128)(2,1)} %bitcast.8), calls=%async_computation.2 | async-start | bytes 4718592 | tf_op jit(solution)/shard_map/column_gather/all_to_all | solution.py:249
  85.4 1.0 collective-permute-done.9.refs_6_
  86.4 12.8 %collective-permute-done.8.refs_5_ = bf16[16,128,128]{2,1,0:T(8,128)(2,1)} collective-permute-done((bf16[16,128,128]{2,1,0:T(8,128)(2,1)S(1)}, bf16[16,128,128]{2,1,0:T(8,128)(2,1)}, u32[]{:S(2)}, u32[]{:S(2)}) %collective-permute-start.8) | collective-permute-done | bytes 524320 | tf_op jit(solution)/shard_map/column_gather/ppermute | solution.py:253
  99.2 1.9 %collective-permute-done.7.refs_4_ = bf16[16,128,128]{2,1,0:T(8,128)(2,1)} collective-permute-done((bf16[16,128,128]{2,1,0:T(8,128)(2,1)S(1)}, bf16[16,128,128]{2,1,0:T(8,128)(2,1)}, u32[]{:S(2)}, u32[]{:S(2)}) %collective-permute-start.7) | collective-permute-done | bytes 524320 | tf_op jit(solution)/shard_map/column_gather/ppermute | solution.py:253
  101.1 2.9 %collective-permute-start.10 = (bf16[64,128,128]{2,1,0:T(8,128)(2,1)}, bf16[64,128,128]{2,1,0:T(8,128)(2,1)}, u32[]{:S(2)}, u32[]{:S(2)}) collective-permute-start(bf16[64,128,128]{2,1,0:T(8,128)(2,1)} %all-gather.2.cloned.1.call-done.refs_1_), channel_id=1, source_target_pairs={{0,16},{16,0},{32,48},{48,32},{64,80},{80,64},{96,112},{112,96},{1... | collective-permute-start | bytes 6291464 | tf_op jit(solution)/shard_map/core_swap/ppermute | solution.py:288
  103.9 3.0 %all-to-all-done.2.refs_0_ = bf16[72,128,128]{2,1,0:T(8,128)(2,1)S(1)} async-done(((bf16[72,128,128]{2,1,0:T(8,128)(2,1)}), bf16[72,128,128]{2,1,0:T(8,128)(2,1)S(1)}, u32[]{:S(2)}, u32[]{:S(2)}) %all-to-all-start.2) | async-done | bytes 2359328 | tf_op jit(solution)/shard_map/column_gather/all_to_all | solution.py:249
  106.9 1.4 copy-done.2
  108.4 8.8 %collective-permute-start.11 = (bf16[4,128,128]{2,1,0:T(8,128)(2,1)S(1)}, bf16[4,128,128]{2,1,0:T(8,128)(2,1)S(1)}, u32[]{:S(2)}, u32[]{:S(2)}) collective-permute-start(bf16[4,128,128]{2,1,0:T(8,128)(2,1)S(1)} %pad_maximum_fusion.2), channel_id=1, source_target_pairs={{0,16},{16,0},{32,48},{48,32},{64,80},{80,64},{96,112},{112,96},{1... | collective-permute-start | bytes 393224 | tf_op jit(solution)/shard_map/core_swap/ppermute | solution.py:289
  117.2 0.7 pad_add_fusion.me
  117.9 0.3 collective-permute-done.11.refs_8_
  118.2 0.0 collective-permute-done.10.refs_2_
  118.2 0.0 copy-done.4
  118.2 0.6 copy-done.5
  118.8 25.1 %update.1 = bf16[128,128,128]{2,1,0:T(8,128)(2,1)} custom-call(s32[2,128]{1,0:T(2,128)} %bitcast.5, s32[2]{0:T(128)} %pad_add_fusion.me, s32[2,256]{1,0:T(2,128)} %pivots.1, bf16[2,256,256]{2,1,0:T(8,128)(2,1)} %inverses.1, bf16[72,128,128]{2,1,0:T(8,128)(2,1)} %copy-done.2, bf16[64,128,128]{2,1,0:T(8,128)(2,1)} %all-gather.2.cloned.1.call-done.refs_1_, ...), custom_call_target="tpu_custom_call" | custom-call | tf_op jit(solution)/shard_map/update/pallas_call | solution.py:229
  (17 shorter events, 0.2 us)
Async XLA Ops:
  6.5 2.2 %copy-start = (bf16[128,128,128]{2,1,0:T(8,128)(2,1)S(1)}, bf16[128,128,128]{2,1,0:T(8,128)(2,1)}, u32[]{:S(2)}) copy-start(bf16[128,128,128]{2,1,0:T(8,128)(2,1)} %refs_7_.1) | copy-start | bytes 12582916
  8.7 0.7 copy-start.1
  13.0 28.5 %collective-permute-start = (bf16[10,128,128]{2,1,0:T(8,128)(2,1)S(1)}, bf16[10,128,128]{2,1,0:T(8,128)(2,1)}, u32[]{:S(2)}, u32[]{:S(2)}) collective-permute-start(bf16[10,128,128]{2,1,0:T(8,128)(2,1)S(1)} %get-tuple-element.13), channel_id=1, source_target_pairs={{0,192},{16,208},{32,224},{48,240},{1,193},{17,209},{33,225},{49,2... | collective-permute-start | bytes 983048 | tf_op jit(solution)/shard_map/row_scatter/ppermute | solution.py:267
  21.2 20.3 %collective-permute-start.1 = (bf16[10,128,128]{2,1,0:T(8,128)(2,1)S(1)}, bf16[10,128,128]{2,1,0:T(8,128)(2,1)}, u32[]{:S(2)}, u32[]{:S(2)}) collective-permute-start(bf16[10,128,128]{2,1,0:T(8,128)(2,1)S(1)} %get-tuple-element.14), channel_id=1, source_target_pairs={{0,128},{16,144},{32,160},{48,176},{1,129},{17,145},{33,161},{49,1... | collective-permute-start | bytes 983048 | tf_op jit(solution)/shard_map/row_scatter/ppermute | solution.py:267
  23.5 18.0 %collective-permute-start.2 = (bf16[10,128,128]{2,1,0:T(8,128)(2,1)S(1)}, bf16[10,128,128]{2,1,0:T(8,128)(2,1)}, u32[]{:S(2)}, u32[]{:S(2)}) collective-permute-start(bf16[10,128,128]{2,1,0:T(8,128)(2,1)S(1)} %get-tuple-element.15), channel_id=1, source_target_pairs={{0,64},{16,80},{32,96},{48,112},{1,65},{17,81},{33,97},{49,113},{2... | collective-permute-start | bytes 983048 | tf_op jit(solution)/shard_map/row_scatter/ppermute | solution.py:267
  30.0 32.4 %all-to-all-start = ((bf16[64,128,128]{2,1,0:T(8,128)(2,1)}), bf16[64,128,128]{2,1,0:T(8,128)(2,1)S(1)}, u32[]{:S(2)}, u32[]{:S(2)}) async-start(bf16[64,128,128]{2,1,0:T(8,128)(2,1)} %extract_columns.1), calls=%async_computation | async-start | bytes 4194304 | tf_op jit(solution)/shard_map/column_scatter/all_to_all | solution.py:270
  36.3 64.8 %all-gather.2.cloned.1.call-start = ((), (), s32[]{:S(2)}) async-start(), calls=%async_computation.3 | async-start | bytes 2359296 | tf_op jit(solution)/shard_map/row_gather/all_gather | solution.py:272
  42.3 5.3 %collective-permute-start.3 = (bf16[2,128,128]{2,1,0:T(8,128)(2,1)S(1)}, bf16[2,128,128]{2,1,0:T(8,128)(2,1)S(1)}, u32[]{:S(2)}, u32[]{:S(2)}) collective-permute-start(bf16[2,128,128]{2,1,0:T(8,128)(2,1)S(1)} %slice.45), channel_id=1, source_target_pairs={{0,32},{16,48},{32,64},{48,80},{64,96},{80,112},{96,128},{112,144}... | collective-permute-start | bytes 196616 | tf_op jit(solution)/shard_map/corner_gather/ppermute | solution.py:277
  63.5 11.8 %all-to-all-start.1 = ((bf16[24,128,128]{2,1,0:T(8,128)(2,1)}), bf16[24,128,128]{2,1,0:T(8,128)(2,1)S(1)}, u32[]{:S(2)}, u32[]{:S(2)}) async-start(bf16[24,128,128]{2,1,0:T(8,128)(2,1)} %bitcast.3), calls=%async_computation.1 | async-start | bytes 1572864 | tf_op jit(solution)/shard_map/column_gather/all_to_all | solution.py:249
  67.0 5.4 %collective-permute-start.6 = (bf16[4,128,128]{2,1,0:T(8,128)(2,1)S(1)}, bf16[4,128,128]{2,1,0:T(8,128)(2,1)S(1)}, u32[]{:S(2)}, u32[]{:S(2)}) collective-permute-start(bf16[4,128,128]{2,1,0:T(8,128)(2,1)S(1)} %get-tuple-element.21), channel_id=1, source_target_pairs={{0,2},{1,3},{2,0},{3,1},{4,6},{5,7},{6,4},{7,5},{8,10},{9,11},{10,... | collective-permute-start | bytes 393224 | tf_op jit(solution)/shard_map/column_gather/ppermute | solution.py:253
  69.2 4.2 %collective-permute-start.5 = (bf16[4,128,128]{2,1,0:T(8,128)(2,1)S(1)}, bf16[4,128,128]{2,1,0:T(8,128)(2,1)S(1)}, u32[]{:S(2)}, u32[]{:S(2)}) collective-permute-start(bf16[4,128,128]{2,1,0:T(8,128)(2,1)S(1)} %get-tuple-element.21), channel_id=1, source_target_pairs={{0,3},{1,0},{2,1},{3,2},{4,7},{5,4},{6,5},{7,6},{8,11},{9,8},{10,9... | collective-permute-start | bytes 393224 | tf_op jit(solution)/shard_map/column_gather/ppermute | solution.py:253
  69.8 5.4 %collective-permute-start.4 = (bf16[4,128,128]{2,1,0:T(8,128)(2,1)S(1)}, bf16[4,128,128]{2,1,0:T(8,128)(2,1)S(1)}, u32[]{:S(2)}, u32[]{:S(2)}) collective-permute-start(bf16[4,128,128]{2,1,0:T(8,128)(2,1)S(1)} %get-tuple-element.21), channel_id=1, source_target_pairs={{0,1},{1,2},{2,3},{3,0},{4,5},{5,6},{6,7},{7,4},{8,9},{9,10},{10,1... | collective-permute-start | bytes 393224 | tf_op jit(solution)/shard_map/column_gather/ppermute | solution.py:253
  75.3 6.5 %copy-start.3 = (bf16[16,128,128]{2,1,0:T(8,128)(2,1)}, bf16[16,128,128]{2,1,0:T(8,128)(2,1)S(1)}, u32[]{:S(2)}) copy-start(bf16[16,128,128]{2,1,0:T(8,128)(2,1)S(1)} %pad_maximum_fusion.refs_3_) | copy-start | bytes 1572868
  75.3 11.1 %collective-permute-start.9 = (bf16[16,128,128]{2,1,0:T(8,128)(2,1)S(1)}, bf16[16,128,128]{2,1,0:T(8,128)(2,1)S(1)}, u32[]{:S(2)}, u32[]{:S(2)}) collective-permute-start(bf16[16,128,128]{2,1,0:T(8,128)(2,1)S(1)} %pad_maximum_fusion.refs_3_), channel_id=1, source_target_pairs={{0,8},{1,9},{2,10},{3,11},{4,12},{5,13},{6,14},{7,15},{8,0},{9,1},... | collective-permute-start | bytes 1572872 | tf_op jit(solution)/shard_map/column_gather/ppermute | solution.py:253
  78.2 20.9 %collective-permute-start.8 = (bf16[16,128,128]{2,1,0:T(8,128)(2,1)S(1)}, bf16[16,128,128]{2,1,0:T(8,128)(2,1)}, u32[]{:S(2)}, u32[]{:S(2)}) collective-permute-start(bf16[16,128,128]{2,1,0:T(8,128)(2,1)S(1)} %pad_maximum_fusion.refs_3_), channel_id=1, source_target_pairs={{0,12},{1,13},{2,14},{3,15},{4,0},{5,1},{6,2},{7,3},{8,4},{9,5},{1... | collective-permute-start | bytes 1572872 | tf_op jit(solution)/shard_map/column_gather/ppermute | solution.py:253
  79.1 22.0 %collective-permute-start.7 = (bf16[16,128,128]{2,1,0:T(8,128)(2,1)S(1)}, bf16[16,128,128]{2,1,0:T(8,128)(2,1)}, u32[]{:S(2)}, u32[]{:S(2)}) collective-permute-start(bf16[16,128,128]{2,1,0:T(8,128)(2,1)S(1)} %pad_maximum_fusion.refs_3_), channel_id=1, source_target_pairs={{0,4},{1,5},{2,6},{3,7},{4,8},{5,9},{6,10},{7,11},{8,12},{9,13},{1... | collective-permute-start | bytes 1572872 | tf_op jit(solution)/shard_map/column_gather/ppermute | solution.py:253
  81.8 25.1 %all-to-all-start.2 = ((bf16[72,128,128]{2,1,0:T(8,128)(2,1)}), bf16[72,128,128]{2,1,0:T(8,128)(2,1)S(1)}, u32[]{:S(2)}, u32[]{:S(2)}) async-start(bf16[72,128,128]{2,1,0:T(8,128)(2,1)} %bitcast.8), calls=%async_computation.2 | async-start | bytes 4718592 | tf_op jit(solution)/shard_map/column_gather/all_to_all | solution.py:249
  86.4 31.8 %copy-start.4 = (bf16[16,128,128]{2,1,0:T(8,128)(2,1)}, bf16[16,128,128]{2,1,0:T(8,128)(2,1)S(1)}, u32[]{:S(2)}) copy-start(bf16[16,128,128]{2,1,0:T(8,128)(2,1)S(1)} %collective-permute-done.9.refs_6_) | copy-start | bytes 1572868
  101.1 17.1 %collective-permute-start.10 = (bf16[64,128,128]{2,1,0:T(8,128)(2,1)}, bf16[64,128,128]{2,1,0:T(8,128)(2,1)}, u32[]{:S(2)}, u32[]{:S(2)}) collective-permute-start(bf16[64,128,128]{2,1,0:T(8,128)(2,1)} %all-gather.2.cloned.1.call-done.refs_1_), channel_id=1, source_target_pairs={{0,16},{16,0},{32,48},{48,32},{64,80},{80,64},{96,112},{112,96},{1... | collective-permute-start | bytes 6291464 | tf_op jit(solution)/shard_map/core_swap/ppermute | solution.py:288
  106.9 1.4 copy-start.2
  108.4 9.8 %collective-permute-start.11 = (bf16[4,128,128]{2,1,0:T(8,128)(2,1)S(1)}, bf16[4,128,128]{2,1,0:T(8,128)(2,1)S(1)}, u32[]{:S(2)}, u32[]{:S(2)}) collective-permute-start(bf16[4,128,128]{2,1,0:T(8,128)(2,1)S(1)} %pad_maximum_fusion.2), channel_id=1, source_target_pairs={{0,16},{16,0},{32,48},{48,32},{64,80},{80,64},{96,112},{112,96},{1... | collective-permute-start | bytes 393224 | tf_op jit(solution)/shard_map/core_swap/ppermute | solution.py:289
  118.2 0.7 copy-start.5
Sparse Core Ops, SparseCore 0:
  42.4 41.0 all-gather.1

commit v4 on v3

--- a/solution.py
+++ b/solution.py
@@ -102,8 +102,8 @@
     fetches = [
         pltpu.make_async_copy(a, b, in_sem.at[n]) for n, (a, b) in enumerate(zip(sources, held))
     ]
-    for fetch in fetches:
-        fetch.start()
+    for n in (8, 0, 1, 2, 3, 4, 5, 6, 7):
+        fetches[n].start()
     panel0, rows_mine, rows_other, *panel1, tiles, corner_other = held
     p, q = me[0], me[1]
     c = p % 2

time: 151 us -> 148 us (0.980)
  Pallas kernels: 33.1 us -> 30.3 us
    pallas_call x1, Pallas kernels: 25.1 us -> 22.2 us  [update(): pl.pallas_call(update_kernel, out_shape=jax.ShapeDtypeStruct((SLOTS, T, T...]
where the time goes in v4:
time: 148 us
  starting transfers between devices  49.6 us (34%)
  waiting for transfers between devices  44.8 us (30%)
  Pallas kernels  30.3 us (20%)
  between operations  13.6 us (9%)
  local copies, waits for them, and re-layouts  8.83 us (6%)
    pallas_call x1, Pallas kernels, update(): pl.pallas_call(update_kernel, out_shape=jax.ShapeDtypeStruct((SLOTS, T, T...  22.2 us
    ppermute x6, waiting for transfers between devices, around(): return [piece] + [lax.ppermute(piece, 'pcol', move(d)) for d in (1, -1, 2)]  20.2 us
    all_to_all x1, waiting for transfers between devices, local(): shards = lax.all_to_all(col, 'pcol', 0, 0, tiled=True)  14.7 us
    ppermute x3, starting transfers between devices, local(): got = lax.ppermute(quarters[m], 'prow', scatter_z(m))  12.5 us
    ppermute x1, starting transfers between devices, local(): lax.ppermute(jnp.concatenate([panel0[16:18], panel0[34:36]]), 'prow', SWAP)  8.83 us
    ppermute x6, starting transfers between devices, around(): return [piece] + [lax.ppermute(piece, 'pcol', move(d)) for d in (1, -1, 2)]  8.01 us
    all_to_all x2, starting transfers between devices, spread(): lax.all_to_all(copies, 'pcol', 0, 0, tiled=True, axis_index_groups=groups)  7.13 us
    all_to_all x1, starting transfers between devices, local(): shards = lax.all_to_all(col, 'pcol', 0, 0, tiled=True)  6.28 us
  transfers between devices with their start and end apart: 16, of which 12 were waited for; matrix products, arithmetic and copies ran while one was open for 3% of the time, Pallas kernels for 3%

profile of v4, /device:TPU:1, one launch (start us, length us, event | category | flops | bytes accessed | tf_op | source)
XLA Modules:
  0.0 147.9 jit_solution(12107030743469900046)
XLA Ops:
  6.5 2.2 %copy-done = bf16[128,128,128]{2,1,0:T(8,128)(2,1)S(1)} copy-done((bf16[128,128,128]{2,1,0:T(8,128)(2,1)S(1)}, bf16[128,128,128]{2,1,0:T(8,128)(2,1)}, u32[]{:S(2)}) %copy-start) | copy-done | bytes 4194328
  8.7 0.7 copy-done.1
  9.4 3.6 %extract_rows.1 = (bf16[10,128,128]{2,1,0:T(8,128)(2,1)S(1)}, bf16[10,128,128]{2,1,0:T(8,128)(2,1)S(1)}, bf16[10,128,128]{2,1,0:T(8,128)(2,1)S(1)}, bf16[10,128,128]{2,1,0:T(8,128)(2,1)S(1)}) custom-call(s32[2,128]{1,0:T(2,128)S(1)} %bitcast.6, bf16[128,128,128]{2,1,0:T(8,128)(2,1)S(1)} %copy-done), custom_call_target="tpu_custom_call" | custom-call | tf_op jit(solution)/shard_map/extract_rows/pallas_call | solution.py:85
  13.0 8.2 %collective-permute-start = (bf16[10,128,128]{2,1,0:T(8,128)(2,1)S(1)}, bf16[10,128,128]{2,1,0:T(8,128)(2,1)}, u32[]{:S(2)}, u32[]{:S(2)}) collective-permute-start(bf16[10,128,128]{2,1,0:T(8,128)(2,1)S(1)} %get-tuple-element.13), channel_id=1, source_target_pairs={{0,192},{16,208},{32,224},{48,240},{1,193},{17,209},{33,225},{49,2... | collective-permute-start | bytes 983048 | tf_op jit(solution)/shard_map/row_scatter/ppermute | solution.py:267
  21.2 2.3 %collective-permute-start.1 = (bf16[10,128,128]{2,1,0:T(8,128)(2,1)S(1)}, bf16[10,128,128]{2,1,0:T(8,128)(2,1)}, u32[]{:S(2)}, u32[]{:S(2)}) collective-permute-start(bf16[10,128,128]{2,1,0:T(8,128)(2,1)S(1)} %get-tuple-element.14), channel_id=1, source_target_pairs={{0,128},{16,144},{32,160},{48,176},{1,129},{17,145},{33,161},{49,1... | collective-permute-start | bytes 983048 | tf_op jit(solution)/shard_map/row_scatter/ppermute | solution.py:267
  23.5 2.0 %collective-permute-start.2 = (bf16[10,128,128]{2,1,0:T(8,128)(2,1)S(1)}, bf16[10,128,128]{2,1,0:T(8,128)(2,1)}, u32[]{:S(2)}, u32[]{:S(2)}) collective-permute-start(bf16[10,128,128]{2,1,0:T(8,128)(2,1)S(1)} %get-tuple-element.15), channel_id=1, source_target_pairs={{0,64},{16,80},{32,96},{48,112},{1,65},{17,81},{33,97},{49,113},{2... | collective-permute-start | bytes 983048 | tf_op jit(solution)/shard_map/row_scatter/ppermute | solution.py:267
  25.5 4.5 %extract_columns.1 = bf16[64,128,128]{2,1,0:T(8,128)(2,1)} custom-call(s32[2,128]{1,0:T(2,128)S(1)} %bitcast.7, bf16[128,128,128]{2,1,0:T(8,128)(2,1)S(1)} %copy-done, bf16[10,128,128]{2,1,0:T(8,128)(2,1)S(1)} %get-tuple-element.12.after), custom_call_target="tpu_custom_call" | custom-call | tf_op jit(solution)/shard_map/extract_columns/pallas_call | solution.py:74
  30.0 6.3 %all-to-all-start = ((bf16[64,128,128]{2,1,0:T(8,128)(2,1)}), bf16[64,128,128]{2,1,0:T(8,128)(2,1)S(1)}, u32[]{:S(2)}, u32[]{:S(2)}) async-start(bf16[64,128,128]{2,1,0:T(8,128)(2,1)} %extract_columns.1), calls=%async_computation | async-start | bytes 4194304 | tf_op jit(solution)/shard_map/column_scatter/all_to_all | solution.py:270
  36.3 0.0 all-gather.2.cloned.1.call-start
  36.3 5.1 %collective-permute-done = bf16[10,128,128]{2,1,0:T(8,128)(2,1)} collective-permute-done((bf16[10,128,128]{2,1,0:T(8,128)(2,1)S(1)}, bf16[10,128,128]{2,1,0:T(8,128)(2,1)}, u32[]{:S(2)}, u32[]{:S(2)}) %collective-permute-start) | collective-permute-done | bytes 327712 | tf_op jit(solution)/shard_map/row_scatter/ppermute | solution.py:267
  41.5 0.0 collective-permute-done.1
  41.5 0.0 collective-permute-done.2
  41.5 0.1 select_select_fusion
  41.5 0.7 slice.47
  42.3 0.0 all-gather.2.cloned.1.call-update
  42.3 4.0 %collective-permute-start.3 = (bf16[2,128,128]{2,1,0:T(8,128)(2,1)S(1)}, bf16[2,128,128]{2,1,0:T(8,128)(2,1)S(1)}, u32[]{:S(2)}, u32[]{:S(2)}) collective-permute-start(bf16[2,128,128]{2,1,0:T(8,128)(2,1)S(1)} %slice.45), channel_id=1, source_target_pairs={{0,32},{16,48},{32,64},{48,80},{64,96},{80,112},{96,128},{112,144}... | collective-permute-start | bytes 196616 | tf_op jit(solution)/shard_map/corner_gather/ppermute | solution.py:277
  46.3 1.3 collective-permute-done.3
  47.6 14.7 %all-to-all-done = bf16[64,128,128]{2,1,0:T(8,128)(2,1)S(1)} async-done(((bf16[64,128,128]{2,1,0:T(8,128)(2,1)}), bf16[64,128,128]{2,1,0:T(8,128)(2,1)S(1)}, u32[]{:S(2)}, u32[]{:S(2)}) %all-to-all-start) | async-done | bytes 2097184 | tf_op jit(solution)/shard_map/column_scatter/all_to_all | solution.py:270
  62.4 1.0 broadcast_in_dim.4
  63.5 3.5 %all-to-all-start.1 = ((bf16[24,128,128]{2,1,0:T(8,128)(2,1)}), bf16[24,128,128]{2,1,0:T(8,128)(2,1)S(1)}, u32[]{:S(2)}, u32[]{:S(2)}) async-start(bf16[24,128,128]{2,1,0:T(8,128)(2,1)} %bitcast.3), calls=%async_computation.1 | async-start | bytes 1572864 | tf_op jit(solution)/shard_map/column_gather/all_to_all | solution.py:249
  67.0 2.2 %collective-permute-start.6 = (bf16[4,128,128]{2,1,0:T(8,128)(2,1)S(1)}, bf16[4,128,128]{2,1,0:T(8,128)(2,1)S(1)}, u32[]{:S(2)}, u32[]{:S(2)}) collective-permute-start(bf16[4,128,128]{2,1,0:T(8,128)(2,1)S(1)} %get-tuple-element.21), channel_id=1, source_target_pairs={{0,2},{1,3},{2,0},{3,1},{4,6},{5,7},{6,4},{7,5},{8,10},{9,11},{10,... | collective-permute-start | bytes 393224 | tf_op jit(solution)/shard_map/column_gather/ppermute | solution.py:253
  69.2 0.6 collective-permute-start.5
  69.8 0.9 collective-permute-start.4
  70.7 1.7 %collective-permute-done.6 = bf16[4,128,128]{2,1,0:T(8,128)(2,1)S(1)} collective-permute-done((bf16[4,128,128]{2,1,0:T(8,128)(2,1)S(1)}, bf16[4,128,128]{2,1,0:T(8,128)(2,1)S(1)}, u32[]{:S(2)}, u32[]{:S(2)}) %collective-permute-start.6) | collective-permute-done | bytes 131104 | tf_op jit(solution)/shard_map/column_gather/ppermute | solution.py:253
  72.4 1.0 collective-permute-done.5
  73.4 1.8 %collective-permute-done.4 = bf16[4,128,128]{2,1,0:T(8,128)(2,1)S(1)} collective-permute-done((bf16[4,128,128]{2,1,0:T(8,128)(2,1)S(1)}, bf16[4,128,128]{2,1,0:T(8,128)(2,1)S(1)}, u32[]{:S(2)}, u32[]{:S(2)}) %collective-permute-start.4) | collective-permute-done | bytes 131104 | tf_op jit(solution)/shard_map/column_gather/ppermute | solution.py:253
  75.2 0.1 pad_maximum_fusion.refs_3_
  75.3 0.0 copy-start.3
  75.3 0.1 all-to-all-done.1
  75.3 2.9 %collective-permute-start.9 = (bf16[16,128,128]{2,1,0:T(8,128)(2,1)S(1)}, bf16[16,128,128]{2,1,0:T(8,128)(2,1)S(1)}, u32[]{:S(2)}, u32[]{:S(2)}) collective-permute-start(bf16[16,128,128]{2,1,0:T(8,128)(2,1)S(1)} %pad_maximum_fusion.refs_3_), channel_id=1, source_target_pairs={{0,8},{1,9},{2,10},{3,11},{4,12},{5,13},{6,14},{7,15},{8,0},{9,1},... | collective-permute-start | bytes 1572872 | tf_op jit(solution)/shard_map/column_gather/ppermute | solution.py:253
  78.2 0.9 collective-permute-start.8
  79.1 0.6 collective-permute-start.7
  79.8 2.0 %broadcast_in_dim.5 = bf16[4,18,128,128]{3,2,1,0:T(8,128)(2,1)} broadcast(bf16[18,128,128]{2,1,0:T(8,128)(2,1)S(1)} %slice_dynamic-update-slice_fusion.4), dimensions={1,2,3} | broadcast | bytes 2949120 | tf_op jit(solution)/shard_map/column_gather/broadcast_in_dim | solution.py:248
  81.8 0.0 copy-done.3
  81.8 3.6 %all-to-all-start.2 = ((bf16[72,128,128]{2,1,0:T(8,128)(2,1)}), bf16[72,128,128]{2,1,0:T(8,128)(2,1)S(1)}, u32[]{:S(2)}, u32[]{:S(2)}) async-start(bf16[72,128,128]{2,1,0:T(8,128)(2,1)} %bitcast.8), calls=%async_computation.2 | async-start | bytes 4718592 | tf_op jit(solution)/shard_map/column_gather/all_to_all | solution.py:249
  85.4 1.0 collective-permute-done.9.refs_6_
  86.4 12.8 %collective-permute-done.8.refs_5_ = bf16[16,128,128]{2,1,0:T(8,128)(2,1)} collective-permute-done((bf16[16,128,128]{2,1,0:T(8,128)(2,1)S(1)}, bf16[16,128,128]{2,1,0:T(8,128)(2,1)}, u32[]{:S(2)}, u32[]{:S(2)}) %collective-permute-start.8) | collective-permute-done | bytes 524320 | tf_op jit(solution)/shard_map/column_gather/ppermute | solution.py:253
  99.2 1.9 %collective-permute-done.7.refs_4_ = bf16[16,128,128]{2,1,0:T(8,128)(2,1)} collective-permute-done((bf16[16,128,128]{2,1,0:T(8,128)(2,1)S(1)}, bf16[16,128,128]{2,1,0:T(8,128)(2,1)}, u32[]{:S(2)}, u32[]{:S(2)}) %collective-permute-start.7) | collective-permute-done | bytes 524320 | tf_op jit(solution)/shard_map/column_gather/ppermute | solution.py:253
  101.1 2.9 %collective-permute-start.10 = (bf16[64,128,128]{2,1,0:T(8,128)(2,1)}, bf16[64,128,128]{2,1,0:T(8,128)(2,1)}, u32[]{:S(2)}, u32[]{:S(2)}) collective-permute-start(bf16[64,128,128]{2,1,0:T(8,128)(2,1)} %all-gather.2.cloned.1.call-done.refs_1_), channel_id=1, source_target_pairs={{0,16},{16,0},{32,48},{48,32},{64,80},{80,64},{96,112},{112,96},{1... | collective-permute-start | bytes 6291464 | tf_op jit(solution)/shard_map/core_swap/ppermute | solution.py:288
  103.9 3.0 %all-to-all-done.2.refs_0_ = bf16[72,128,128]{2,1,0:T(8,128)(2,1)S(1)} async-done(((bf16[72,128,128]{2,1,0:T(8,128)(2,1)}), bf16[72,128,128]{2,1,0:T(8,128)(2,1)S(1)}, u32[]{:S(2)}, u32[]{:S(2)}) %all-to-all-start.2) | async-done | bytes 2359328 | tf_op jit(solution)/shard_map/column_gather/all_to_all | solution.py:249
  106.9 1.4 copy-done.2
  108.4 8.8 %collective-permute-start.11 = (bf16[4,128,128]{2,1,0:T(8,128)(2,1)S(1)}, bf16[4,128,128]{2,1,0:T(8,128)(2,1)S(1)}, u32[]{:S(2)}, u32[]{:S(2)}) collective-permute-start(bf16[4,128,128]{2,1,0:T(8,128)(2,1)S(1)} %pad_maximum_fusion.2), channel_id=1, source_target_pairs={{0,16},{16,0},{32,48},{48,32},{64,80},{80,64},{96,112},{112,96},{1... | collective-permute-start | bytes 393224 | tf_op jit(solution)/shard_map/core_swap/ppermute | solution.py:289
  117.2 0.7 pad_add_fusion.me
  117.9 0.3 collective-permute-done.11.refs_8_
  118.2 0.0 collective-permute-done.10.refs_2_
  118.2 0.0 copy-done.4
  118.2 0.6 copy-done.5
  118.8 22.2 %update.1 = bf16[128,128,128]{2,1,0:T(8,128)(2,1)} custom-call(s32[2,128]{1,0:T(2,128)} %bitcast.5, s32[2]{0:T(128)} %pad_add_fusion.me, s32[2,256]{1,0:T(2,128)} %pivots.1, bf16[2,256,256]{2,1,0:T(8,128)(2,1)} %inverses.1, bf16[72,128,128]{2,1,0:T(8,128)(2,1)} %copy-done.2, bf16[64,128,128]{2,1,0:T(8,128)(2,1)} %all-gather.2.cloned.1.call-done.refs_1_, ...), custom_call_target="tpu_custom_call" | custom-call | tf_op jit(solution)/shard_map/update/pallas_call | solution.py:229
  (17 shorter events, 0.2 us)
Async XLA Ops:
  6.5 2.2 %copy-start = (bf16[128,128,128]{2,1,0:T(8,128)(2,1)S(1)}, bf16[128,128,128]{2,1,0:T(8,128)(2,1)}, u32[]{:S(2)}) copy-start(bf16[128,128,128]{2,1,0:T(8,128)(2,1)} %refs_7_.1) | copy-start | bytes 12582916
  8.7 0.7 copy-start.1
  13.0 28.5 %collective-permute-start = (bf16[10,128,128]{2,1,0:T(8,128)(2,1)S(1)}, bf16[10,128,128]{2,1,0:T(8,128)(2,1)}, u32[]{:S(2)}, u32[]{:S(2)}) collective-permute-start(bf16[10,128,128]{2,1,0:T(8,128)(2,1)S(1)} %get-tuple-element.13), channel_id=1, source_target_pairs={{0,192},{16,208},{32,224},{48,240},{1,193},{17,209},{33,225},{49,2... | collective-permute-start | bytes 983048 | tf_op jit(solution)/shard_map/row_scatter/ppermute | solution.py:267
  21.2 20.3 %collective-permute-start.1 = (bf16[10,128,128]{2,1,0:T(8,128)(2,1)S(1)}, bf16[10,128,128]{2,1,0:T(8,128)(2,1)}, u32[]{:S(2)}, u32[]{:S(2)}) collective-permute-start(bf16[10,128,128]{2,1,0:T(8,128)(2,1)S(1)} %get-tuple-element.14), channel_id=1, source_target_pairs={{0,128},{16,144},{32,160},{48,176},{1,129},{17,145},{33,161},{49,1... | collective-permute-start | bytes 983048 | tf_op jit(solution)/shard_map/row_scatter/ppermute | solution.py:267
  23.5 18.0 %collective-permute-start.2 = (bf16[10,128,128]{2,1,0:T(8,128)(2,1)S(1)}, bf16[10,128,128]{2,1,0:T(8,128)(2,1)}, u32[]{:S(2)}, u32[]{:S(2)}) collective-permute-start(bf16[10,128,128]{2,1,0:T(8,128)(2,1)S(1)} %get-tuple-element.15), channel_id=1, source_target_pairs={{0,64},{16,80},{32,96},{48,112},{1,65},{17,81},{33,97},{49,113},{2... | collective-permute-start | bytes 983048 | tf_op jit(solution)/shard_map/row_scatter/ppermute | solution.py:267
  30.0 32.4 %all-to-all-start = ((bf16[64,128,128]{2,1,0:T(8,128)(2,1)}), bf16[64,128,128]{2,1,0:T(8,128)(2,1)S(1)}, u32[]{:S(2)}, u32[]{:S(2)}) async-start(bf16[64,128,128]{2,1,0:T(8,128)(2,1)} %extract_columns.1), calls=%async_computation | async-start | bytes 4194304 | tf_op jit(solution)/shard_map/column_scatter/all_to_all | solution.py:270
  36.3 64.8 %all-gather.2.cloned.1.call-start = ((), (), s32[]{:S(2)}) async-start(), calls=%async_computation.3 | async-start | bytes 2359296 | tf_op jit(solution)/shard_map/row_gather/all_gather | solution.py:272
  42.3 5.3 %collective-permute-start.3 = (bf16[2,128,128]{2,1,0:T(8,128)(2,1)S(1)}, bf16[2,128,128]{2,1,0:T(8,128)(2,1)S(1)}, u32[]{:S(2)}, u32[]{:S(2)}) collective-permute-start(bf16[2,128,128]{2,1,0:T(8,128)(2,1)S(1)} %slice.45), channel_id=1, source_target_pairs={{0,32},{16,48},{32,64},{48,80},{64,96},{80,112},{96,128},{112,144}... | collective-permute-start | bytes 196616 | tf_op jit(solution)/shard_map/corner_gather/ppermute | solution.py:277
  63.5 11.8 %all-to-all-start.1 = ((bf16[24,128,128]{2,1,0:T(8,128)(2,1)}), bf16[24,128,128]{2,1,0:T(8,128)(2,1)S(1)}, u32[]{:S(2)}, u32[]{:S(2)}) async-start(bf16[24,128,128]{2,1,0:T(8,128)(2,1)} %bitcast.3), calls=%async_computation.1 | async-start | bytes 1572864 | tf_op jit(solution)/shard_map/column_gather/all_to_all | solution.py:249
  67.0 5.4 %collective-permute-start.6 = (bf16[4,128,128]{2,1,0:T(8,128)(2,1)S(1)}, bf16[4,128,128]{2,1,0:T(8,128)(2,1)S(1)}, u32[]{:S(2)}, u32[]{:S(2)}) collective-permute-start(bf16[4,128,128]{2,1,0:T(8,128)(2,1)S(1)} %get-tuple-element.21), channel_id=1, source_target_pairs={{0,2},{1,3},{2,0},{3,1},{4,6},{5,7},{6,4},{7,5},{8,10},{9,11},{10,... | collective-permute-start | bytes 393224 | tf_op jit(solution)/shard_map/column_gather/ppermute | solution.py:253
  69.2 4.2 %collective-permute-start.5 = (bf16[4,128,128]{2,1,0:T(8,128)(2,1)S(1)}, bf16[4,128,128]{2,1,0:T(8,128)(2,1)S(1)}, u32[]{:S(2)}, u32[]{:S(2)}) collective-permute-start(bf16[4,128,128]{2,1,0:T(8,128)(2,1)S(1)} %get-tuple-element.21), channel_id=1, source_target_pairs={{0,3},{1,0},{2,1},{3,2},{4,7},{5,4},{6,5},{7,6},{8,11},{9,8},{10,9... | collective-permute-start | bytes 393224 | tf_op jit(solution)/shard_map/column_gather/ppermute | solution.py:253
  69.8 5.4 %collective-permute-start.4 = (bf16[4,128,128]{2,1,0:T(8,128)(2,1)S(1)}, bf16[4,128,128]{2,1,0:T(8,128)(2,1)S(1)}, u32[]{:S(2)}, u32[]{:S(2)}) collective-permute-start(bf16[4,128,128]{2,1,0:T(8,128)(2,1)S(1)} %get-tuple-element.21), channel_id=1, source_target_pairs={{0,1},{1,2},{2,3},{3,0},{4,5},{5,6},{6,7},{7,4},{8,9},{9,10},{10,1... | collective-permute-start | bytes 393224 | tf_op jit(solution)/shard_map/column_gather/ppermute | solution.py:253
  75.3 6.5 %copy-start.3 = (bf16[16,128,128]{2,1,0:T(8,128)(2,1)}, bf16[16,128,128]{2,1,0:T(8,128)(2,1)S(1)}, u32[]{:S(2)}) copy-start(bf16[16,128,128]{2,1,0:T(8,128)(2,1)S(1)} %pad_maximum_fusion.refs_3_) | copy-start | bytes 1572868
  75.3 11.1 %collective-permute-start.9 = (bf16[16,128,128]{2,1,0:T(8,128)(2,1)S(1)}, bf16[16,128,128]{2,1,0:T(8,128)(2,1)S(1)}, u32[]{:S(2)}, u32[]{:S(2)}) collective-permute-start(bf16[16,128,128]{2,1,0:T(8,128)(2,1)S(1)} %pad_maximum_fusion.refs_3_), channel_id=1, source_target_pairs={{0,8},{1,9},{2,10},{3,11},{4,12},{5,13},{6,14},{7,15},{8,0},{9,1},... | collective-permute-start | bytes 1572872 | tf_op jit(solution)/shard_map/column_gather/ppermute | solution.py:253
  78.2 20.9 %collective-permute-start.8 = (bf16[16,128,128]{2,1,0:T(8,128)(2,1)S(1)}, bf16[16,128,128]{2,1,0:T(8,128)(2,1)}, u32[]{:S(2)}, u32[]{:S(2)}) collective-permute-start(bf16[16,128,128]{2,1,0:T(8,128)(2,1)S(1)} %pad_maximum_fusion.refs_3_), channel_id=1, source_target_pairs={{0,12},{1,13},{2,14},{3,15},{4,0},{5,1},{6,2},{7,3},{8,4},{9,5},{1... | collective-permute-start | bytes 1572872 | tf_op jit(solution)/shard_map/column_gather/ppermute | solution.py:253
  79.1 22.0 %collective-permute-start.7 = (bf16[16,128,128]{2,1,0:T(8,128)(2,1)S(1)}, bf16[16,128,128]{2,1,0:T(8,128)(2,1)}, u32[]{:S(2)}, u32[]{:S(2)}) collective-permute-start(bf16[16,128,128]{2,1,0:T(8,128)(2,1)S(1)} %pad_maximum_fusion.refs_3_), channel_id=1, source_target_pairs={{0,4},{1,5},{2,6},{3,7},{4,8},{5,9},{6,10},{7,11},{8,12},{9,13},{1... | collective-permute-start | bytes 1572872 | tf_op jit(solution)/shard_map/column_gather/ppermute | solution.py:253
  81.8 25.1 %all-to-all-start.2 = ((bf16[72,128,128]{2,1,0:T(8,128)(2,1)}), bf16[72,128,128]{2,1,0:T(8,128)(2,1)S(1)}, u32[]{:S(2)}, u32[]{:S(2)}) async-start(bf16[72,128,128]{2,1,0:T(8,128)(2,1)} %bitcast.8), calls=%async_computation.2 | async-start | bytes 4718592 | tf_op jit(solution)/shard_map/column_gather/all_to_all | solution.py:249
  86.4 31.8 %copy-start.4 = (bf16[16,128,128]{2,1,0:T(8,128)(2,1)}, bf16[16,128,128]{2,1,0:T(8,128)(2,1)S(1)}, u32[]{:S(2)}) copy-start(bf16[16,128,128]{2,1,0:T(8,128)(2,1)S(1)} %collective-permute-done.9.refs_6_) | copy-start | bytes 1572868
  101.1 17.1 %collective-permute-start.10 = (bf16[64,128,128]{2,1,0:T(8,128)(2,1)}, bf16[64,128,128]{2,1,0:T(8,128)(2,1)}, u32[]{:S(2)}, u32[]{:S(2)}) collective-permute-start(bf16[64,128,128]{2,1,0:T(8,128)(2,1)} %all-gather.2.cloned.1.call-done.refs_1_), channel_id=1, source_target_pairs={{0,16},{16,0},{32,48},{48,32},{64,80},{80,64},{96,112},{112,96},{1... | collective-permute-start | bytes 6291464 | tf_op jit(solution)/shard_map/core_swap/ppermute | solution.py:288
  106.9 1.4 copy-start.2
  108.4 9.8 %collective-permute-start.11 = (bf16[4,128,128]{2,1,0:T(8,128)(2,1)S(1)}, bf16[4,128,128]{2,1,0:T(8,128)(2,1)S(1)}, u32[]{:S(2)}, u32[]{:S(2)}) collective-permute-start(bf16[4,128,128]{2,1,0:T(8,128)(2,1)S(1)} %pad_maximum_fusion.2), channel_id=1, source_target_pairs={{0,16},{16,0},{32,48},{48,32},{64,80},{80,64},{96,112},{112,96},{1... | collective-permute-start | bytes 393224 | tf_op jit(solution)/shard_map/core_swap/ppermute | solution.py:289
  118.2 0.7 copy-start.5
Sparse Core Ops, SparseCore 0:
  42.4 41.0 all-gather.1
